TPU v7x, 512 devices: a whole 4x8x8 slice. The times are simulated.
512 devices in a mesh: tm: 16 (over z, core), space: 32 (over y, x).
Axes of the slice: x: 4, y: 8, z: 8, core: 2. Of those that a mesh axis runs over, the one named last changes fastest.
Arguments:
- increments: float32 [16, 8, 256, 1440], P('tm', None, 'space'), may hold values from -6 to 6
- background: float32 [8, 256, 1440], P(None, 'space'), may hold values from -6 to 6
- error_weight: float32 [8, 256, 1440], P(None, 'space'), may hold values from 0.5 to 2
- neighbor_weights: float32 [4, 256, 1440], P(None, 'space'), may hold values from 0.03 to 0.24
- operators: bfloat16 [16, 4, 768, 128, 128], P('tm', None, 'space'), may hold values from -0.5 to 0.5
- values: float32 [16, 4, 768, 128], P('tm', None, 'space'), may hold values from -6 to 6
- obs_weight: float32 [16, 4, 768, 128], P('tm', None, 'space'), may hold values from 0.3 to 3
- owners: int32 [16, 4, 768, 1], P('tm', None, 'space'), may hold values from 0 to 31; in each aligned block of 24 rows (0 to 23, 24 to 47, ..., all dimensions but the last counted through in order) at most 2 rows name the same one
- columns: int32 [16, 4, 768], P('tm', None, 'space'), may hold values from 0 to 719
Outputs:
- gradient: float32 [16, 8, 256, 1440], P('tm', None, 'space')
- departures: float32 [16, 4, 768, 128], P('tm', None, 'space')
Inputs may be any that keep to these rules, and one draw needn't show every extreme that they name: `owners`: among the 24 observation blocks of one step that one slab holds, at most 2 name the same owner slab, and in some such groups exactly 2 do.
All inputs are finite; a program needn't handle non-finite values.
Results may differ from a plain program's by a relative error of at most 0.003.
Values may be sent and summed in bfloat16 or wider, within the bound.
No kernel may reach another device: no remote copies, remote signals or barrier semaphores. Data moves between devices by JAX's collectives and lax.ppermute only.
A program may use at most 64 MiB of HBM per device.

v0:
```python
import jax
import jax.numpy as jnp
from jax import lax
from jax.sharding import PartitionSpec as P


def with_halo(cells, sides, width):
    for axis, dim in sides:
        count = lax.axis_size(axis)
        ends = count - 1
        head = lax.slice_in_dim(cells, 0, width, axis=dim)
        tail = lax.slice_in_dim(cells, cells.shape[dim] - width, cells.shape[dim], axis=dim)
        cells = jnp.concatenate(
            [
                lax.ppermute(tail, axis, [(i, (i + 1) % count) for i in range(ends)]),
                cells,
                lax.ppermute(head, axis, [((i + 1) % count, i) for i in range(ends)]),
            ],
            axis=dim,
        )
    return cells


def passed_along(block, axis, distance):
    devices = range(lax.axis_size(axis))
    route = [(i - distance, i) for i in devices if i - distance in devices]
    return lax.ppermute(block, axis, route)


def lat_rims(stacked):
    return with_halo(stacked, (("space", 2),), 1)


def forward_step(field, coeffs):
    east, west, north, south = (coeffs[0], coeffs[1], coeffs[2], coeffs[3])
    center = 1.0 - (east + west + north + south)
    padded = lat_rims(field[None])[0]
    return (
        center * field
        + east * jnp.roll(field, -1, -1)
        + west * jnp.roll(field, 1, -1)
        + north * padded[:, 2:, :]
        + south * padded[:, :-2, :]
    )


def adjoint_step(adjoint, coeffs):
    east, west, north, south = (coeffs[0], coeffs[1], coeffs[2], coeffs[3])
    center = 1.0 - (east + west + north + south)
    padded = lat_rims(jnp.stack([north * adjoint, south * adjoint]))
    return (
        center * adjoint
        + jnp.roll(east * adjoint, 1, -1)
        + jnp.roll(west * adjoint, -1, -1)
        + padded[0][:, :-2, :]
        + padded[1][:, 2:, :]
    )


def slot_table(owner, column, slots_per, parts):
    count = owner.shape[0]
    order = jnp.arange(count, dtype=jnp.int32)
    before = (owner[:, None] == owner[None, :]) & (order[None, :] < order[:, None])
    rank = jnp.sum(before.astype(jnp.int32), axis=1)
    slot = owner * slots_per + rank
    select = (slot[:, None] == jnp.arange(parts * slots_per, dtype=jnp.int32)[None, :]).astype(
        jnp.int32
    )
    request = jnp.sum(select * column[:, None], axis=0).reshape(parts, slots_per)
    return (select, request)


def fetch(request, table):
    received = lax.all_to_all(request, "space", split_axis=0, concat_axis=0, tiled=True)
    blocks = jnp.take(table, received, axis=0)
    return (lax.all_to_all(blocks, "space", split_axis=0, concat_axis=0, tiled=True), received)


def observe(select, fetched, ops, observed, weights):
    picked = jnp.dot(
        select.astype(jnp.bfloat16), fetched, preferred_element_type=jnp.float32
    ).astype(jnp.bfloat16)
    departure = jnp.einsum("oab,ob->oa", ops, picked, preferred_element_type=jnp.float32) - observed
    scaled = (weights * departure).astype(jnp.bfloat16)
    increment = jnp.einsum("oab,oa->ob", ops, scaled, preferred_element_type=jnp.float32)
    slots = jnp.dot(select.astype(jnp.float32).T, increment, precision=lax.Precision.HIGHEST)
    return (departure, slots)


def deliver(slots, received, total_rows):
    arrived = lax.all_to_all(slots, "space", split_axis=0, concat_axis=0, tiled=True)
    width = arrived.shape[-1]
    picker = (
        received.reshape(-1)[:, None] == jnp.arange(total_rows, dtype=jnp.int32)[None, :]
    ).astype(jnp.float32)
    return jnp.dot(picker.T, arrived.reshape(-1, width), precision=lax.Precision.HIGHEST)


def local(
    increments,
    background,
    error_weight,
    neighbor_weights,
    operators,
    values,
    obs_weight,
    owners,
    columns,
):
    start_field = increments[0]
    parts = lax.axis_size("space")
    steps = operators.shape[1]
    count = operators.shape[2]
    width = operators.shape[3]
    slots_per = max(2, 2 * count // parts)
    rows = start_field.size // width
    first_window = lax.axis_index("tm") == 0
    states = []
    field = start_field
    for step in range(steps):
        field = forward_step(field, neighbor_weights)
        states.append(field)
    previous = passed_along(field.astype(jnp.bfloat16), "tm", 1).astype(field.dtype)
    begin = jnp.where(first_window, background, previous)
    weighted = error_weight * (start_field - begin)
    adjoint = -passed_along(weighted.astype(jnp.bfloat16), "tm", -1).astype(weighted.dtype)
    tables = [state.astype(jnp.bfloat16).reshape(rows, width) for state in states]
    selects = []
    requests = []
    for step in range(steps):
        select, request = slot_table(owners[0, step, :, 0], columns[0, step], slots_per, parts)
        selects.append(select)
        requests.append(request)
    departures = []
    forcing = []
    for step in range(steps):
        fetched, received = fetch(requests[step], tables[step])
        departure, slots = observe(
            selects[step],
            fetched.reshape(-1, width),
            operators[0, step],
            values[0, step],
            obs_weight[0, step],
        )
        departures.append(departure)
        added = deliver(slots.reshape(parts, slots_per, width), received, rows)
        forcing.append(added.reshape(start_field.shape))
    for step in range(steps - 1, -1, -1):
        adjoint = adjoint_step(adjoint + forcing[step], neighbor_weights)
    gradient = weighted + adjoint
    return (gradient[None], jnp.stack(departures, 0)[None])


def solution(mesh):
    in_specs = (
        P("tm", None, "space", None),
        P(None, "space", None),
        P(None, "space", None),
        P(None, "space", None),
        P("tm", None, "space", None, None),
        P("tm", None, "space", None),
        P("tm", None, "space", None),
        P("tm", None, "space", None),
        P("tm", None, "space"),
    )
    out_specs = (P("tm", None, "space", None), P("tm", None, "space", None))
    return jax.shard_map(local, mesh=mesh, in_specs=in_specs, out_specs=out_specs, check_vma=False)
```

profile of v0, /device:TPU:286, one launch (start us, length us, event | category | flops | bytes accessed | tf_op | source)
XLA Modules:
  0.0 263.6 jit_solution(5611051049473317956)
XLA Ops:
  1.9 4.6 %collective-permute-start = (f32[1,8,1,1440]{3,2,1,0:T(1,128)S(1)}, f32[1,8,1,1440]{3,2,1,0:T(1,128)S(1)}, u32[]{:S(2)}, u32[]{:S(2)}) collective-permute-start(f32[1,8,1,1440]{3,2,1,0:T(1,128)S(1)} %get-tuple-element.68), channel_id=1, source_target_pairs={{0,1},{1,2},{2,3},{3,4},{4,5},{5,6},{6,7},{7,8},{8,9},{9,10},{10,1... | collective-permute-start | bytes 138248 | tf_op jit(solution)/shard_map/ppermute | solution.py:15
  12.3 10.0 %all-to-all-start = ((s32[32,1,2]{2,1,0:T(1,128)}), s32[32,1,2]{2,1,0:T(1,128)S(1)}, u32[]{:S(2)}, u32[]{:S(2)}) async-start(s32[32,1,2]{2,1,0:T(1,128)} %bitcast.15), calls=%async_computation | async-start | bytes 32768 | tf_op jit(solution)/shard_map/all_to_all | solution.py:74
  27.6 8.2 %all-to-all-start.3 = ((s32[32,1,2]{2,1,0:T(1,128)}), s32[32,1,2]{2,1,0:T(1,128)S(1)}, u32[]{:S(2)}, u32[]{:S(2)}) async-start(s32[32,1,2]{2,1,0:T(1,128)} %bitcast.36), calls=%async_computation.3 | async-start | bytes 32768 | tf_op jit(solution)/shard_map/all_to_all | solution.py:74
  35.9 5.2 %all-to-all-done.3 = s32[32,1,2]{2,1,0:T(1,128)S(1)} async-done(((s32[32,1,2]{2,1,0:T(1,128)}), s32[32,1,2]{2,1,0:T(1,128)S(1)}, u32[]{:S(2)}, u32[]{:S(2)}) %all-to-all-start.3) | async-done | bytes 288 | tf_op jit(solution)/shard_map/all_to_all | solution.py:74
  41.1 8.2 %all-to-all-start.6 = ((s32[32,1,2]{2,1,0:T(1,128)}), s32[32,1,2]{2,1,0:T(1,128)S(1)}, u32[]{:S(2)}, u32[]{:S(2)}) async-start(s32[32,1,2]{2,1,0:T(1,128)} %bitcast.57), calls=%async_computation.6 | async-start | bytes 32768 | tf_op jit(solution)/shard_map/all_to_all | solution.py:74
  49.4 5.3 %all-to-all-done.6 = s32[32,1,2]{2,1,0:T(1,128)S(1)} async-done(((s32[32,1,2]{2,1,0:T(1,128)}), s32[32,1,2]{2,1,0:T(1,128)S(1)}, u32[]{:S(2)}, u32[]{:S(2)}) %all-to-all-start.6) | async-done | bytes 288 | tf_op jit(solution)/shard_map/all_to_all | solution.py:74
  54.7 8.1 %all-to-all-start.9 = ((s32[32,1,2]{2,1,0:T(1,128)}), s32[32,1,2]{2,1,0:T(1,128)S(1)}, u32[]{:S(2)}, u32[]{:S(2)}) async-start(s32[32,1,2]{2,1,0:T(1,128)} %bitcast.78), calls=%async_computation.9 | async-start | bytes 32768 | tf_op jit(solution)/shard_map/all_to_all | solution.py:74
  62.9 5.3 %all-to-all-done.9 = s32[32,1,2]{2,1,0:T(1,128)S(1)} async-done(((s32[32,1,2]{2,1,0:T(1,128)}), s32[32,1,2]{2,1,0:T(1,128)S(1)}, u32[]{:S(2)}, u32[]{:S(2)}) %all-to-all-start.9) | async-done | bytes 288 | tf_op jit(solution)/shard_map/all_to_all | solution.py:74
  75.7 8.2 %all-to-all-start.10 = ((bf16[32,2,128]{2,1,0:T(2,128)(2,1)}), bf16[32,2,128]{2,1,0:T(2,128)(2,1)S(1)}, u32[]{:S(2)}, u32[]{:S(2)}) async-start(bf16[32,2,128]{2,1,0:T(2,128)(2,1)} %broadcast_select_fusion), calls=%async_computation.10 | async-start | bytes 32768 | tf_op jit(solution)/shard_map/all_to_all | solution.py:76
  84.0 4.6 %collective-permute-start.2 = (f32[1,8,1,1440]{3,2,1,0:T(1,128)S(1)}, f32[1,8,1,1440]{3,2,1,0:T(1,128)S(1)}, u32[]{:S(2)}, u32[]{:S(2)}) collective-permute-start(f32[1,8,1,1440]{3,2,1,0:T(1,128)S(1)} %get-tuple-element.62), channel_id=1, source_target_pairs={{0,1},{1,2},{2,3},{3,4},{4,5},{5,6},{6,7},{7,8},{8,9},{9,10},{10,1... | collective-permute-start | bytes 138248 | tf_op jit(solution)/shard_map/ppermute | solution.py:15
  88.6 1.9 collective-permute-start.3
  92.3 5.5 %collective-permute-done.3 = f32[1,8,1,1440]{3,2,1,0:T(1,128)S(1)} collective-permute-done((f32[1,8,1,1440]{3,2,1,0:T(1,128)S(1)}, f32[1,8,1,1440]{3,2,1,0:T(1,128)S(1)}, u32[]{:S(2)}, u32[]{:S(2)}) %collective-permute-start.3) | collective-permute-done | bytes 46112 | tf_op jit(solution)/shard_map/ppermute | solution.py:17
  100.3 7.4 %all-to-all-start.7 = ((bf16[32,2,128]{2,1,0:T(2,128)(2,1)}), bf16[32,2,128]{2,1,0:T(2,128)(2,1)S(1)}, u32[]{:S(2)}, u32[]{:S(2)}) async-start(bf16[32,2,128]{2,1,0:T(2,128)(2,1)} %broadcast_select_fusion.1), calls=%async_computation.7 | async-start | bytes 32768 | tf_op jit(solution)/shard_map/all_to_all | solution.py:76
  107.7 4.6 %collective-permute-start.4 = (f32[1,8,1,1440]{3,2,1,0:T(1,128)S(1)}, f32[1,8,1,1440]{3,2,1,0:T(1,128)S(1)}, u32[]{:S(2)}, u32[]{:S(2)}) collective-permute-start(f32[1,8,1,1440]{3,2,1,0:T(1,128)S(1)} %get-tuple-element.56), channel_id=1, source_target_pairs={{0,1},{1,2},{2,3},{3,4},{4,5},{5,6},{6,7},{7,8},{8,9},{9,10},{10,1... | collective-permute-start | bytes 138248 | tf_op jit(solution)/shard_map/ppermute | solution.py:15
  116.1 5.5 %collective-permute-done.5 = f32[1,8,1,1440]{3,2,1,0:T(1,128)S(1)} collective-permute-done((f32[1,8,1,1440]{3,2,1,0:T(1,128)S(1)}, f32[1,8,1,1440]{3,2,1,0:T(1,128)S(1)}, u32[]{:S(2)}, u32[]{:S(2)}) %collective-permute-start.5) | collective-permute-done | bytes 46112 | tf_op jit(solution)/shard_map/ppermute | solution.py:17
  124.0 7.4 %all-to-all-start.4 = ((bf16[32,2,128]{2,1,0:T(2,128)(2,1)}), bf16[32,2,128]{2,1,0:T(2,128)(2,1)S(1)}, u32[]{:S(2)}, u32[]{:S(2)}) async-start(bf16[32,2,128]{2,1,0:T(2,128)(2,1)} %broadcast_select_fusion.2), calls=%async_computation.4 | async-start | bytes 32768 | tf_op jit(solution)/shard_map/all_to_all | solution.py:76
  131.5 4.6 %collective-permute-start.6 = (f32[1,8,1,1440]{3,2,1,0:T(1,128)S(1)}, f32[1,8,1,1440]{3,2,1,0:T(1,128)S(1)}, u32[]{:S(2)}, u32[]{:S(2)}) collective-permute-start(f32[1,8,1,1440]{3,2,1,0:T(1,128)S(1)} %get-tuple-element.50), channel_id=1, source_target_pairs={{0,1},{1,2},{2,3},{3,4},{4,5},{5,6},{6,7},{7,8},{8,9},{9,10},{10,1... | collective-permute-start | bytes 138248 | tf_op jit(solution)/shard_map/ppermute | solution.py:15
  136.1 1.9 collective-permute-start.7
  138.2 7.2 %collective-permute-done.7 = f32[1,8,1,1440]{3,2,1,0:T(1,128)S(1)} collective-permute-done((f32[1,8,1,1440]{3,2,1,0:T(1,128)S(1)}, f32[1,8,1,1440]{3,2,1,0:T(1,128)S(1)}, u32[]{:S(2)}, u32[]{:S(2)}) %collective-permute-start.7) | collective-permute-done | bytes 46112 | tf_op jit(solution)/shard_map/ppermute | solution.py:17
  147.5 7.4 %all-to-all-start.1 = ((bf16[32,2,128]{2,1,0:T(2,128)(2,1)}), bf16[32,2,128]{2,1,0:T(2,128)(2,1)S(1)}, u32[]{:S(2)}, u32[]{:S(2)}) async-start(bf16[32,2,128]{2,1,0:T(2,128)(2,1)} %broadcast_select_fusion.3), calls=%async_computation.1 | async-start | bytes 32768 | tf_op jit(solution)/shard_map/all_to_all | solution.py:76
  156.6 1.9 collective-permute-start.8
  165.0 8.4 %all-to-all-start.2 = ((f32[32,2,128]{2,1,0:T(2,128)}), f32[32,2,128]{2,1,0:T(2,128)S(1)}, u32[]{:S(2)}, u32[]{:S(2)}) async-start(f32[32,2,128]{2,1,0:T(2,128)} %bitcast.28), calls=%async_computation.2 | async-start | bytes 65536 | tf_op jit(solution)/shard_map/all_to_all | solution.py:91
  181.3 4.0 %collective-permute-start.9 = (bf16[8,8,1440]{2,1,0:T(8,128)(2,1)S(1)}, bf16[8,8,1440]{2,1,0:T(8,128)(2,1)S(1)}, u32[]{:S(2)}, u32[]{:S(2)}) collective-permute-start(bf16[8,8,1440]{2,1,0:T(8,128)(2,1)S(1)} %get-tuple-element.9), channel_id=1, source_target_pairs={{32,0},{64,32},{96,64},{128,96},{160,128},{192,160},{224,192},{256... | collective-permute-start | bytes 552968 | tf_op jit(solution)/shard_map/ppermute | solution.py:27
  185.3 9.8 %all-to-all-start.5 = ((f32[32,2,128]{2,1,0:T(2,128)}), f32[32,2,128]{2,1,0:T(2,128)S(1)}, u32[]{:S(2)}, u32[]{:S(2)}) async-start(f32[32,2,128]{2,1,0:T(2,128)} %bitcast.49), calls=%async_computation.5 | async-start | bytes 65536 | tf_op jit(solution)/shard_map/all_to_all | solution.py:91
  196.9 4.6 %collective-permute-start.10 = (f32[2,8,1,1440]{3,2,1,0:T(1,128)}, f32[2,8,1,1440]{3,2,1,0:T(1,128)S(1)}, u32[]{:S(2)}, u32[]{:S(2)}) collective-permute-start(f32[2,8,1,1440]{3,2,1,0:T(1,128)} %get-tuple-element.31), channel_id=1, source_target_pairs={{0,1},{1,2},{2,3},{3,4},{4,5},{5,6},{6,7},{7,8},{8,9},{9,10},{10,1... | collective-permute-start | bytes 276488 | tf_op jit(solution)/shard_map/ppermute | solution.py:15
  203.4 10.0 %all-to-all-start.8 = ((f32[32,2,128]{2,1,0:T(2,128)}), f32[32,2,128]{2,1,0:T(2,128)S(1)}, u32[]{:S(2)}, u32[]{:S(2)}) async-start(f32[32,2,128]{2,1,0:T(2,128)} %bitcast.70), calls=%async_computation.8 | async-start | bytes 65536 | tf_op jit(solution)/shard_map/all_to_all | solution.py:91
  215.5 4.6 %collective-permute-start.12 = (f32[2,8,1,1440]{3,2,1,0:T(1,128)S(1)}, f32[2,8,1,1440]{3,2,1,0:T(1,128)S(1)}, u32[]{:S(2)}, u32[]{:S(2)}) collective-permute-start(f32[2,8,1,1440]{3,2,1,0:T(1,128)S(1)} %get-tuple-element.29), channel_id=1, source_target_pairs={{0,1},{1,2},{2,3},{3,4},{4,5},{5,6},{6,7},{7,8},{8,9},{9,10},{10,1... | collective-permute-start | bytes 276488 | tf_op jit(solution)/shard_map/ppermute | solution.py:15
  222.1 10.0 %all-to-all-start.11 = ((f32[32,2,128]{2,1,0:T(2,128)}), f32[32,2,128]{2,1,0:T(2,128)S(1)}, u32[]{:S(2)}, u32[]{:S(2)}) async-start(f32[32,2,128]{2,1,0:T(2,128)} %bitcast.91), calls=%async_computation.11 | async-start | bytes 65536 | tf_op jit(solution)/shard_map/all_to_all | solution.py:91
  234.2 4.6 %collective-permute-start.14 = (f32[2,8,1,1440]{3,2,1,0:T(1,128)S(1)}, f32[2,8,1,1440]{3,2,1,0:T(1,128)S(1)}, u32[]{:S(2)}, u32[]{:S(2)}) collective-permute-start(f32[2,8,1,1440]{3,2,1,0:T(1,128)S(1)} %get-tuple-element.27), channel_id=1, source_target_pairs={{0,1},{1,2},{2,3},{3,4},{4,5},{5,6},{6,7},{7,8},{8,9},{9,10},{10,1... | collective-permute-start | bytes 276488 | tf_op jit(solution)/shard_map/ppermute | solution.py:15
  241.8 6.8 %collective-permute-done.15 = f32[2,8,1,1440]{3,2,1,0:T(1,128)S(1)} collective-permute-done((f32[2,8,1,1440]{3,2,1,0:T(1,128)S(1)}, f32[2,8,1,1440]{3,2,1,0:T(1,128)S(1)}, u32[]{:S(2)}, u32[]{:S(2)}) %collective-permute-start.15) | collective-permute-done | bytes 92192 | tf_op jit(solution)/shard_map/ppermute | solution.py:17
  251.5 3.9 %collective-permute-start.17 = (f32[2,8,1,1440]{3,2,1,0:T(1,128)S(1)}, f32[2,8,1,1440]{3,2,1,0:T(1,128)S(1)}, u32[]{:S(2)}, u32[]{:S(2)}) collective-permute-start(f32[2,8,1,1440]{3,2,1,0:T(1,128)S(1)} %get-tuple-element.26), channel_id=1, source_target_pairs={{1,0},{2,1},{3,2},{4,3},{5,4},{6,5},{7,6},{8,7},{9,8},{10,9},{11,1... | collective-permute-start | bytes 276488 | tf_op jit(solution)/shard_map/ppermute | solution.py:17
  256.3 5.0 %collective-permute-done.17 = f32[2,8,1,1440]{3,2,1,0:T(1,128)S(1)} collective-permute-done((f32[2,8,1,1440]{3,2,1,0:T(1,128)S(1)}, f32[2,8,1,1440]{3,2,1,0:T(1,128)S(1)}, u32[]{:S(2)}, u32[]{:S(2)}) %collective-permute-start.17) | collective-permute-done | bytes 92192 | tf_op jit(solution)/shard_map/ppermute | solution.py:17
  (188 shorter events, 67.4 us)
Async XLA Ops:
  0.6 23.1 %copy-start = (f32[1,8,8,1440]{3,2,1,0:T(8,128)S(1)}, f32[1,8,8,1440]{3,2,1,0:T(8,128)}, u32[]{:S(2)}) copy-start(f32[1,8,8,1440]{3,2,1,0:T(8,128)} %param.11) | copy-start | bytes 1105924
  0.6 23.1 %copy-start.4 = (f32[4,8,1440]{2,1,0:T(8,128)S(1)}, f32[4,8,1440]{2,1,0:T(8,128)}, u32[]{:S(2)}) copy-start(f32[4,8,1440]{2,1,0:T(8,128)} %param.14) | copy-start | bytes 552964
  1.9 71.3 %collective-permute-start = (f32[1,8,1,1440]{3,2,1,0:T(1,128)S(1)}, f32[1,8,1,1440]{3,2,1,0:T(1,128)S(1)}, u32[]{:S(2)}, u32[]{:S(2)}) collective-permute-start(f32[1,8,1,1440]{3,2,1,0:T(1,128)S(1)} %get-tuple-element.68), channel_id=1, source_target_pairs={{0,1},{1,2},{2,3},{3,4},{4,5},{5,6},{6,7},{7,8},{8,9},{9,10},{10,1... | collective-permute-start | bytes 138248 | tf_op jit(solution)/shard_map/ppermute | solution.py:15
  6.6 66.7 %collective-permute-start.1 = (f32[1,8,1,1440]{3,2,1,0:T(1,128)S(1)}, f32[1,8,1,1440]{3,2,1,0:T(1,128)S(1)}, u32[]{:S(2)}, u32[]{:S(2)}) collective-permute-start(f32[1,8,1,1440]{3,2,1,0:T(1,128)S(1)} %get-tuple-element.69), channel_id=1, source_target_pairs={{1,0},{2,1},{3,2},{4,3},{5,4},{6,5},{7,6},{8,7},{9,8},{10,9},{11,1... | collective-permute-start | bytes 138248 | tf_op jit(solution)/shard_map/ppermute | solution.py:17
  12.3 15.3 %all-to-all-start = ((s32[32,1,2]{2,1,0:T(1,128)}), s32[32,1,2]{2,1,0:T(1,128)S(1)}, u32[]{:S(2)}, u32[]{:S(2)}) async-start(s32[32,1,2]{2,1,0:T(1,128)} %bitcast.15), calls=%async_computation | async-start | bytes 32768 | tf_op jit(solution)/shard_map/all_to_all | solution.py:74
  27.6 13.5 %all-to-all-start.3 = ((s32[32,1,2]{2,1,0:T(1,128)}), s32[32,1,2]{2,1,0:T(1,128)S(1)}, u32[]{:S(2)}, u32[]{:S(2)}) async-start(s32[32,1,2]{2,1,0:T(1,128)} %bitcast.36), calls=%async_computation.3 | async-start | bytes 32768 | tf_op jit(solution)/shard_map/all_to_all | solution.py:74
  41.1 13.6 %all-to-all-start.6 = ((s32[32,1,2]{2,1,0:T(1,128)}), s32[32,1,2]{2,1,0:T(1,128)S(1)}, u32[]{:S(2)}, u32[]{:S(2)}) async-start(s32[32,1,2]{2,1,0:T(1,128)} %bitcast.57), calls=%async_computation.6 | async-start | bytes 32768 | tf_op jit(solution)/shard_map/all_to_all | solution.py:74
  54.7 13.5 %all-to-all-start.9 = ((s32[32,1,2]{2,1,0:T(1,128)}), s32[32,1,2]{2,1,0:T(1,128)S(1)}, u32[]{:S(2)}, u32[]{:S(2)}) async-start(s32[32,1,2]{2,1,0:T(1,128)} %bitcast.78), calls=%async_computation.9 | async-start | bytes 32768 | tf_op jit(solution)/shard_map/all_to_all | solution.py:74
  75.7 14.8 %all-to-all-start.10 = ((bf16[32,2,128]{2,1,0:T(2,128)(2,1)}), bf16[32,2,128]{2,1,0:T(2,128)(2,1)S(1)}, u32[]{:S(2)}, u32[]{:S(2)}) async-start(bf16[32,2,128]{2,1,0:T(2,128)(2,1)} %broadcast_select_fusion), calls=%async_computation.10 | async-start | bytes 32768 | tf_op jit(solution)/shard_map/all_to_all | solution.py:76
  84.0 8.3 %collective-permute-start.2 = (f32[1,8,1,1440]{3,2,1,0:T(1,128)S(1)}, f32[1,8,1,1440]{3,2,1,0:T(1,128)S(1)}, u32[]{:S(2)}, u32[]{:S(2)}) collective-permute-start(f32[1,8,1,1440]{3,2,1,0:T(1,128)S(1)} %get-tuple-element.62), channel_id=1, source_target_pairs={{0,1},{1,2},{2,3},{3,4},{4,5},{5,6},{6,7},{7,8},{8,9},{9,10},{10,1... | collective-permute-start | bytes 138248 | tf_op jit(solution)/shard_map/ppermute | solution.py:15
  88.6 9.3 %collective-permute-start.3 = (f32[1,8,1,1440]{3,2,1,0:T(1,128)S(1)}, f32[1,8,1,1440]{3,2,1,0:T(1,128)S(1)}, u32[]{:S(2)}, u32[]{:S(2)}) collective-permute-start(f32[1,8,1,1440]{3,2,1,0:T(1,128)S(1)} %get-tuple-element.63), channel_id=1, source_target_pairs={{1,0},{2,1},{3,2},{4,3},{5,4},{6,5},{7,6},{8,7},{9,8},{10,9},{11,1... | collective-permute-start | bytes 138248 | tf_op jit(solution)/shard_map/ppermute | solution.py:17
  100.3 14.0 %all-to-all-start.7 = ((bf16[32,2,128]{2,1,0:T(2,128)(2,1)}), bf16[32,2,128]{2,1,0:T(2,128)(2,1)S(1)}, u32[]{:S(2)}, u32[]{:S(2)}) async-start(bf16[32,2,128]{2,1,0:T(2,128)(2,1)} %broadcast_select_fusion.1), calls=%async_computation.7 | async-start | bytes 32768 | tf_op jit(solution)/shard_map/all_to_all | solution.py:76
  107.7 8.3 %collective-permute-start.4 = (f32[1,8,1,1440]{3,2,1,0:T(1,128)S(1)}, f32[1,8,1,1440]{3,2,1,0:T(1,128)S(1)}, u32[]{:S(2)}, u32[]{:S(2)}) collective-permute-start(f32[1,8,1,1440]{3,2,1,0:T(1,128)S(1)} %get-tuple-element.56), channel_id=1, source_target_pairs={{0,1},{1,2},{2,3},{3,4},{4,5},{5,6},{6,7},{7,8},{8,9},{9,10},{10,1... | collective-permute-start | bytes 138248 | tf_op jit(solution)/shard_map/ppermute | solution.py:15
  112.3 9.3 %collective-permute-start.5 = (f32[1,8,1,1440]{3,2,1,0:T(1,128)S(1)}, f32[1,8,1,1440]{3,2,1,0:T(1,128)S(1)}, u32[]{:S(2)}, u32[]{:S(2)}) collective-permute-start(f32[1,8,1,1440]{3,2,1,0:T(1,128)S(1)} %get-tuple-element.57), channel_id=1, source_target_pairs={{1,0},{2,1},{3,2},{4,3},{5,4},{6,5},{7,6},{8,7},{9,8},{10,9},{11,1... | collective-permute-start | bytes 138248 | tf_op jit(solution)/shard_map/ppermute | solution.py:17
  124.0 14.0 %all-to-all-start.4 = ((bf16[32,2,128]{2,1,0:T(2,128)(2,1)}), bf16[32,2,128]{2,1,0:T(2,128)(2,1)S(1)}, u32[]{:S(2)}, u32[]{:S(2)}) async-start(bf16[32,2,128]{2,1,0:T(2,128)(2,1)} %broadcast_select_fusion.2), calls=%async_computation.4 | async-start | bytes 32768 | tf_op jit(solution)/shard_map/all_to_all | solution.py:76
  131.5 6.7 %collective-permute-start.6 = (f32[1,8,1,1440]{3,2,1,0:T(1,128)S(1)}, f32[1,8,1,1440]{3,2,1,0:T(1,128)S(1)}, u32[]{:S(2)}, u32[]{:S(2)}) collective-permute-start(f32[1,8,1,1440]{3,2,1,0:T(1,128)S(1)} %get-tuple-element.50), channel_id=1, source_target_pairs={{0,1},{1,2},{2,3},{3,4},{4,5},{5,6},{6,7},{7,8},{8,9},{9,10},{10,1... | collective-permute-start | bytes 138248 | tf_op jit(solution)/shard_map/ppermute | solution.py:15
  136.1 9.3 %collective-permute-start.7 = (f32[1,8,1,1440]{3,2,1,0:T(1,128)S(1)}, f32[1,8,1,1440]{3,2,1,0:T(1,128)S(1)}, u32[]{:S(2)}, u32[]{:S(2)}) collective-permute-start(f32[1,8,1,1440]{3,2,1,0:T(1,128)S(1)} %get-tuple-element.51), channel_id=1, source_target_pairs={{1,0},{2,1},{3,2},{4,3},{5,4},{6,5},{7,6},{8,7},{9,8},{10,9},{11,1... | collective-permute-start | bytes 138248 | tf_op jit(solution)/shard_map/ppermute | solution.py:17
  147.5 12.6 %all-to-all-start.1 = ((bf16[32,2,128]{2,1,0:T(2,128)(2,1)}), bf16[32,2,128]{2,1,0:T(2,128)(2,1)S(1)}, u32[]{:S(2)}, u32[]{:S(2)}) async-start(bf16[32,2,128]{2,1,0:T(2,128)(2,1)} %broadcast_select_fusion.3), calls=%async_computation.1 | async-start | bytes 32768 | tf_op jit(solution)/shard_map/all_to_all | solution.py:76
  156.6 23.9 %collective-permute-start.8 = (bf16[8,8,1440]{2,1,0:T(8,128)(2,1)S(1)}, bf16[8,8,1440]{2,1,0:T(8,128)(2,1)S(1)}, u32[]{:S(2)}, u32[]{:S(2)}) collective-permute-start(bf16[8,8,1440]{2,1,0:T(8,128)(2,1)S(1)} %fusion.34), channel_id=1, source_target_pairs={{0,32},{32,64},{64,96},{96,128},{128,160},{160,192},{192,224},{224... | collective-permute-start | bytes 552968 | tf_op jit(solution)/shard_map/ppermute | solution.py:27
  165.0 20.3 %all-to-all-start.2 = ((f32[32,2,128]{2,1,0:T(2,128)}), f32[32,2,128]{2,1,0:T(2,128)S(1)}, u32[]{:S(2)}, u32[]{:S(2)}) async-start(f32[32,2,128]{2,1,0:T(2,128)} %bitcast.28), calls=%async_computation.2 | async-start | bytes 65536 | tf_op jit(solution)/shard_map/all_to_all | solution.py:91
  181.3 14.6 %collective-permute-start.9 = (bf16[8,8,1440]{2,1,0:T(8,128)(2,1)S(1)}, bf16[8,8,1440]{2,1,0:T(8,128)(2,1)S(1)}, u32[]{:S(2)}, u32[]{:S(2)}) collective-permute-start(bf16[8,8,1440]{2,1,0:T(8,128)(2,1)S(1)} %get-tuple-element.9), channel_id=1, source_target_pairs={{32,0},{64,32},{96,64},{128,96},{160,128},{192,160},{224,192},{256... | collective-permute-start | bytes 552968 | tf_op jit(solution)/shard_map/ppermute | solution.py:27
  185.3 18.1 %all-to-all-start.5 = ((f32[32,2,128]{2,1,0:T(2,128)}), f32[32,2,128]{2,1,0:T(2,128)S(1)}, u32[]{:S(2)}, u32[]{:S(2)}) async-start(f32[32,2,128]{2,1,0:T(2,128)} %bitcast.49), calls=%async_computation.5 | async-start | bytes 65536 | tf_op jit(solution)/shard_map/all_to_all | solution.py:91
  196.9 17.6 %collective-permute-start.10 = (f32[2,8,1,1440]{3,2,1,0:T(1,128)}, f32[2,8,1,1440]{3,2,1,0:T(1,128)S(1)}, u32[]{:S(2)}, u32[]{:S(2)}) collective-permute-start(f32[2,8,1,1440]{3,2,1,0:T(1,128)} %get-tuple-element.31), channel_id=1, source_target_pairs={{0,1},{1,2},{2,3},{3,4},{4,5},{5,6},{6,7},{7,8},{8,9},{9,10},{10,1... | collective-permute-start | bytes 276488 | tf_op jit(solution)/shard_map/ppermute | solution.py:15
  201.5 13.1 %collective-permute-start.11 = (f32[2,8,1,1440]{3,2,1,0:T(1,128)S(1)}, f32[2,8,1,1440]{3,2,1,0:T(1,128)S(1)}, u32[]{:S(2)}, u32[]{:S(2)}) collective-permute-start(f32[2,8,1,1440]{3,2,1,0:T(1,128)S(1)} %get-tuple-element.32), channel_id=1, source_target_pairs={{1,0},{2,1},{3,2},{4,3},{5,4},{6,5},{7,6},{8,7},{9,8},{10,9},{11,1... | collective-permute-start | bytes 276488 | tf_op jit(solution)/shard_map/ppermute | solution.py:17
  203.4 18.6 %all-to-all-start.8 = ((f32[32,2,128]{2,1,0:T(2,128)}), f32[32,2,128]{2,1,0:T(2,128)S(1)}, u32[]{:S(2)}, u32[]{:S(2)}) async-start(f32[32,2,128]{2,1,0:T(2,128)} %bitcast.70), calls=%async_computation.8 | async-start | bytes 65536 | tf_op jit(solution)/shard_map/all_to_all | solution.py:91
  215.5 17.6 %collective-permute-start.12 = (f32[2,8,1,1440]{3,2,1,0:T(1,128)S(1)}, f32[2,8,1,1440]{3,2,1,0:T(1,128)S(1)}, u32[]{:S(2)}, u32[]{:S(2)}) collective-permute-start(f32[2,8,1,1440]{3,2,1,0:T(1,128)S(1)} %get-tuple-element.29), channel_id=1, source_target_pairs={{0,1},{1,2},{2,3},{3,4},{4,5},{5,6},{6,7},{7,8},{8,9},{9,10},{10,1... | collective-permute-start | bytes 276488 | tf_op jit(solution)/shard_map/ppermute | solution.py:15
  220.1 13.1 %collective-permute-start.13 = (f32[2,8,1,1440]{3,2,1,0:T(1,128)S(1)}, f32[2,8,1,1440]{3,2,1,0:T(1,128)S(1)}, u32[]{:S(2)}, u32[]{:S(2)}) collective-permute-start(f32[2,8,1,1440]{3,2,1,0:T(1,128)S(1)} %get-tuple-element.30), channel_id=1, source_target_pairs={{1,0},{2,1},{3,2},{4,3},{5,4},{6,5},{7,6},{8,7},{9,8},{10,9},{11,1... | collective-permute-start | bytes 276488 | tf_op jit(solution)/shard_map/ppermute | solution.py:17
  222.1 18.6 %all-to-all-start.11 = ((f32[32,2,128]{2,1,0:T(2,128)}), f32[32,2,128]{2,1,0:T(2,128)S(1)}, u32[]{:S(2)}, u32[]{:S(2)}) async-start(f32[32,2,128]{2,1,0:T(2,128)} %bitcast.91), calls=%async_computation.11 | async-start | bytes 65536 | tf_op jit(solution)/shard_map/all_to_all | solution.py:91
  234.2 7.6 %collective-permute-start.14 = (f32[2,8,1,1440]{3,2,1,0:T(1,128)S(1)}, f32[2,8,1,1440]{3,2,1,0:T(1,128)S(1)}, u32[]{:S(2)}, u32[]{:S(2)}) collective-permute-start(f32[2,8,1,1440]{3,2,1,0:T(1,128)S(1)} %get-tuple-element.27), channel_id=1, source_target_pairs={{0,1},{1,2},{2,3},{3,4},{4,5},{5,6},{6,7},{7,8},{8,9},{9,10},{10,1... | collective-permute-start | bytes 276488 | tf_op jit(solution)/shard_map/ppermute | solution.py:15
  238.8 9.8 %collective-permute-start.15 = (f32[2,8,1,1440]{3,2,1,0:T(1,128)S(1)}, f32[2,8,1,1440]{3,2,1,0:T(1,128)S(1)}, u32[]{:S(2)}, u32[]{:S(2)}) collective-permute-start(f32[2,8,1,1440]{3,2,1,0:T(1,128)S(1)} %get-tuple-element.28), channel_id=1, source_target_pairs={{1,0},{2,1},{3,2},{4,3},{5,4},{6,5},{7,6},{8,7},{9,8},{10,9},{11,1... | collective-permute-start | bytes 276488 | tf_op jit(solution)/shard_map/ppermute | solution.py:17
  249.6 6.8 %collective-permute-start.16 = (f32[2,8,1,1440]{3,2,1,0:T(1,128)S(1)}, f32[2,8,1,1440]{3,2,1,0:T(1,128)S(1)}, u32[]{:S(2)}, u32[]{:S(2)}) collective-permute-start(f32[2,8,1,1440]{3,2,1,0:T(1,128)S(1)} %get-tuple-element.25), channel_id=1, source_target_pairs={{0,1},{1,2},{2,3},{3,4},{4,5},{5,6},{6,7},{7,8},{8,9},{9,10},{10,1... | collective-permute-start | bytes 276488 | tf_op jit(solution)/shard_map/ppermute | solution.py:15
  251.5 9.8 %collective-permute-start.17 = (f32[2,8,1,1440]{3,2,1,0:T(1,128)S(1)}, f32[2,8,1,1440]{3,2,1,0:T(1,128)S(1)}, u32[]{:S(2)}, u32[]{:S(2)}) collective-permute-start(f32[2,8,1,1440]{3,2,1,0:T(1,128)S(1)} %get-tuple-element.26), channel_id=1, source_target_pairs={{1,0},{2,1},{3,2},{4,3},{5,4},{6,5},{7,6},{8,7},{9,8},{10,9},{11,1... | collective-permute-start | bytes 276488 | tf_op jit(solution)/shard_map/ppermute | solution.py:17
  (7 other events, 78.5 us)
where the time goes:
time: 265 us; the launch traced here: 264 us
  starting transfers between devices  160 us (60%)
  waiting for transfers between devices  49.1 us (19%)
  matrix products  18.9 us (7%)
  local copies, waits for them, and re-layouts  17.9 us (7%)
  other arithmetic  15.8 us (6%)
    all_to_all x4, starting transfers between devices, deliver(): lax.all_to_all(slots, 'space', split_axis=0, concat_axis=0, tiled=True)  38.3 us
    all_to_all x4, starting transfers between devices, fetch(): lax.all_to_all(request, 'space', split_axis=0, concat_axis=0, tiled=True)  34.6 us
    ppermute x8, starting transfers between devices, with_halo(): lax.ppermute(tail, axis, [(i, (i + 1) % count) for i in range(ends)])  34 us
    all_to_all x4, starting transfers between devices, fetch(): lax.all_to_all(blocks, 'space', split_axis=0, concat_axis=0, tiled=True)  30.3 us
    ppermute x8, waiting for transfers between devices, with_halo(): lax.ppermute(head, axis, [((i + 1) % count, i) for i in range(ends)])  30.1 us
    ppermute x8, starting transfers between devices, with_halo(): lax.ppermute(head, axis, [((i + 1) % count, i) for i in range(ends)])  17.4 us
    all_to_all x4, waiting for transfers between devices, fetch(): lax.all_to_all(request, 'space', split_axis=0, concat_axis=0, tiled=True)  17.3 us
    dot_general x4, matrix products, observe(): jnp.einsum('oab,ob->oa', ops, picked, preferred_element_type=jnp.float32)  6.5 us
  transfers between devices with their start and end apart: 30, of which 10 were waited for; matrix products, arithmetic and copies ran while one was open for 14% of the time, Pallas kernels for 0%

commit v1 on v0

v1 whole, which is shorter than its diff:
```python
import jax
import jax.numpy as jnp
from jax import lax
from jax.experimental import pallas as pl
from jax.experimental.pallas import tpu as pltpu
from jax.sharding import PartitionSpec as P

LEV = 8
ROWS = 8
LON = 1440
WIDE = 1536
PAD = 48
STEPS = 4
HALO = 4
EXT = ROWS + 2 * HALO
OBS = 24
ALL_OBS = STEPS * OBS
BLK = 128
PARTS = 32
SLOTS = 2 * STEPS
SENT = 3 * SLOTS
HALF = 45
BLOCKS = 2 * HALF * LEV
F32 = jnp.float32
BF16 = jnp.bfloat16
I32 = jnp.int32


def iota(shape, dim):
    return lax.broadcasted_iota(I32, shape, dim)


def params(mib):
    return pltpu.CompilerParams(vmem_limit_bytes=int(mib * (1 << 20)))


def copies(sems, *pairs):
    found = [pltpu.make_async_copy(src, dst, sems.at[i]) for i, (src, dst) in enumerate(pairs)]
    for copy in found:
        copy.start()
    return found


def owner_rank(own_ref, step):
    sub, lane = iota((OBS, OBS), 0), iota((OBS, OBS), 1)
    across = jnp.broadcast_to(own_ref[step], (OBS, OBS)).astype(F32)
    down = jnp.sum(jnp.where(sub == lane, across, 0.0), axis=1, keepdims=True)
    same = down == across
    rank_across = jnp.sum(jnp.where(same & (sub < lane), 1.0, 0.0), axis=0, keepdims=True)
    rank_down = jnp.sum(jnp.where(same & (lane < sub), 1.0, 0.0), axis=1, keepdims=True)
    return down, across[:1], rank_down, rank_across


def request_body(own_hbm, col_hbm, out_ref, choice_ref, own_ref, col_ref, sems):
    for copy in copies(sems, (own_hbm, own_ref), (col_hbm, col_ref)):
        copy.wait()
    dest = iota((PARTS, OBS), 0).astype(F32)
    lane = iota((PARTS, BLK), 1)
    line = iota((PARTS, BLK), 0)
    from_lane = iota((OBS, PARTS * SLOTS), 1).astype(F32)
    asked = jnp.zeros((PARTS, BLK), F32)
    sends = [[], [], []]
    picks = []
    for step in range(STEPS):
        down, across, rank_down, rank_across = owner_rank(own_ref, step)
        block = col_ref[pl.ds(step, 1), :]
        group = (block * 1457) >> 16
        row = ((group & 1) * HALF + block - HALF * group) * LEV + (group >> 1)
        value = (row + 1).astype(F32)
        for nth in range(2):
            hit = (across == dest) & (rank_across == float(nth))
            found = jnp.sum(jnp.where(hit, value, 0.0), axis=1, keepdims=True)
            asked = jnp.where(lane == 2 * step + nth, found, asked)
        picks.append(jnp.where(from_lane == down * SLOTS + (2.0 * step) + rank_down, 1.0, 0.0))
        for side, shift in enumerate((0.0, 1.0, -1.0)):
            sends[side].append((across + shift) * SENT + (side * SLOTS + 2.0 * step) + rank_across)
    below = jnp.where(line == 0, 0.0, pltpu.roll(asked, 1, 0))
    above = jnp.where(line == PARTS - 1, 0.0, pltpu.roll(asked, PARTS - 1, 0))
    asked = asked + pltpu.roll(below, SLOTS, 1) + pltpu.roll(above, 2 * SLOTS, 1)
    out_ref[...] = asked.astype(I32) - 1
    pick = jnp.concatenate(picks, axis=0).astype(BF16)
    for half in range(2):
        choice_ref[pl.ds(PARTS * SENT + half * ALL_OBS, ALL_OBS), :] = pick[:, half * BLK : (half + 1) * BLK]
    spare = jnp.full((1, BLK - ALL_OBS), -1.0, F32)
    sends = [jnp.concatenate(parts + [spare], axis=1) for parts in sends]
    slot = iota((SLOTS, BLK), 0).astype(F32)
    for part in range(0, PARTS, 2):
        tiles = []
        for at in (part, part + 1):
            for side in range(3):
                tiles.append(jnp.where(sends[side] == slot + float(at * SENT + side * SLOTS), 1.0, 0.0))
        choice_ref[pl.ds(part * SENT, 2 * SENT), :] = jnp.concatenate(tiles, axis=0).astype(BF16)


def spread(tmp_ref, field):
    for run in range(LON // BLK):
        tmp_ref[run] = field[:, run * BLK : (run + 1) * BLK]
    tail = LON % BLK
    tmp_ref[LON // BLK] = jnp.concatenate(
        [field[:, LON - tail :], field[:, :PAD], field[:, LON - PAD :]], axis=1
    )


def spread_row(tmp_ref, row):
    return jnp.concatenate(
        [tmp_ref[run, pl.ds(row, LEV, stride=ROWS), :] for run in range(WIDE // BLK)], axis=1
    )


def put_row(tmp_ref, row, value):
    for run in range(WIDE // BLK):
        tmp_ref[run, pl.ds(row, LEV, stride=ROWS), :] = value[:, run * BLK : (run + 1) * BLK]


def gathered(tmp_ref):
    return jnp.concatenate([tmp_ref[run] for run in range(WIDE // BLK)], axis=1)[:, :LON]


def edges_body(inc_hbm, wts_hbm, val_hbm, wt_hbm, _, low_ref, high_ref, aux_ref, tmp_ref, inc_ref, wts_ref, sems):
    for copy in copies(
        sems,
        (inc_hbm, inc_ref),
        (wts_hbm, wts_ref),
        (val_hbm, aux_ref.at[pl.ds(0, ALL_OBS)]),
        (wt_hbm, aux_ref.at[pl.ds(ALL_OBS, ALL_OBS)]),
    ):
        copy.wait()
    spread(tmp_ref, inc_ref[...])
    for out_ref, first in ((low_ref, 0), (high_ref, HALO)):
        for row in range(0, HALO, 2):
            pair = [spread_row(tmp_ref, first + row + i)[:, :LON] for i in range(2)]
            out_ref[pl.ds(row * LEV, 2 * LEV), :] = jnp.concatenate(pair, axis=0).astype(BF16)
        rows = [wts_ref[side, first : first + HALO, :] for side in range(4)]
        out_ref[pl.ds(HALO * LEV, 4 * HALO), :] = jnp.concatenate(rows, axis=0).astype(BF16)


def widen(value):
    tail = LON % BLK
    return jnp.concatenate(
        [value[:, : LON - tail], jnp.concatenate([value[:, LON - tail :], value[:, :PAD], value[:, LON - PAD :]], axis=1)],
        axis=1,
    )


def row_of(ref, which, row):
    return jnp.broadcast_to(ref[which, pl.ds(row, 1), :], (LEV, WIDE))


def forward_body(
    inc_hbm, wts_hbm, south_ref, north_ref, table_ref, last_ref, coef_ref,
    x_ref, flat_ref, south_f, north_f, tmp_ref, inc_ref, wts_ref, sems,
):
    waits = copies(sems, (inc_hbm, inc_ref), (wts_hbm, wts_ref))
    south_f[...] = south_ref[...].astype(F32)
    north_f[...] = north_ref[...].astype(F32)
    for row in range(HALO):
        x_ref[row] = widen(south_f[pl.ds(row * LEV, LEV), :])
        x_ref[HALO + ROWS + row] = widen(north_f[pl.ds(row * LEV, LEV), :])
    for copy in waits:
        copy.wait()
    for side in range(4):
        base = HALO * LEV + side * HALO
        coef_ref[side + 1] = widen(
            jnp.concatenate([south_f[base : base + HALO, :], wts_ref[side], north_f[base : base + HALO, :]], axis=0)
        )
    coef_ref[0] = 1.0 - (coef_ref[1] + coef_ref[2] + coef_ref[3] + coef_ref[4])
    spread(tmp_ref, inc_ref[...])
    for row in range(ROWS):
        x_ref[HALO + row] = spread_row(tmp_ref, row)

    for step in range(STEPS):
        old, new = (step % 2) * EXT, ((step + 1) % 2) * EXT
        for row in range(step + 1, EXT - step - 1):
            v = x_ref[old + row]
            moved = (
                row_of(coef_ref, 0, row) * v
                + row_of(coef_ref, 1, row) * pltpu.roll(v, WIDE - 1, 1)
                + row_of(coef_ref, 2, row) * pltpu.roll(v, 1, 1)
                + row_of(coef_ref, 3, row) * x_ref[old + row + 1]
                + row_of(coef_ref, 4, row) * x_ref[old + row - 1]
            )
            x_ref[new + row] = moved
            own = row - HALO
            if 0 <= own < ROWS:
                part = own % 4
                flat_ref[own // 4, :, part * LON : (part + 1) * LON] = moved[:, :LON]
        for pair in range(HALF):
            tiles = []
            for tile in (2 * pair, 2 * pair + 1):
                half, at = tile // HALF, tile % HALF
                tiles.append(flat_ref[half, :, at * BLK : (at + 1) * BLK])
            table_ref[step, pl.ds(pair * 2 * LEV, 2 * LEV), :] = jnp.concatenate(tiles, axis=0).astype(BF16)
    final = (STEPS % 2) * EXT + HALO
    for row in range(ROWS):
        put_row(tmp_ref, row, x_ref[final + row])
    last_ref[...] = gathered(tmp_ref).astype(BF16)


def gather_body(asked_ref, table_ref, _, out_ref, __, slots_ref):
    lane = iota((PARTS, BLOCKS), 1)
    asked = asked_ref[...]
    for step in range(STEPS):
        picks = [
            jnp.where(asked[:, 2 * step + nth : 2 * step + nth + 1] == lane, 1.0, 0.0).astype(BF16)
            for nth in range(2)
        ]
        blocks = jnp.dot(jnp.concatenate(picks, axis=0), table_ref[step], preferred_element_type=F32)
        for nth in range(2):
            slots_ref[pl.ds(2 * step + nth, PARTS, stride=SLOTS), :] = blocks[nth * PARTS : (nth + 1) * PARTS]
    out_ref[...] = slots_ref[...].astype(BF16)


def misfit_body(
    first_ref, inc_hbm, weight_hbm, back_hbm, prev_ref, out_ref, own_ref, low_ref, high_ref, token_ref,
    tmp_ref, inc_ref, weight_ref, back_ref, sems,
):
    for copy in copies(sems, (inc_hbm, inc_ref), (weight_hbm, weight_ref), (back_hbm, back_ref)):
        copy.wait()
    begin = jnp.where(first_ref[0] == 1, back_ref[...], prev_ref[...].astype(F32))
    misfit = weight_ref[...] * (inc_ref[...] - begin)
    out_ref[...] = misfit
    token_ref[...] = misfit[:8, :BLK]
    spread(tmp_ref, misfit)
    for row in range(0, ROWS, 2):
        pair = [spread_row(tmp_ref, row + i)[:, :LON] for i in range(2)]
        both = jnp.concatenate(pair, axis=0).astype(BF16)
        own_ref[pl.ds(row * LEV, 2 * LEV), :] = both
        if row < HALO:
            low_ref[pl.ds(row * LEV, 2 * LEV), :] = both
        else:
            high_ref[pl.ds((row - HALO) * LEV, 2 * LEV), :] = both


def spread_out(block):
    line = iota(block.shape, 0)
    zero = jnp.zeros_like(block)
    return jnp.concatenate([jnp.where(line == i, block, zero) for i in range(block.shape[0])], axis=1)


GROUP = 16


def observe_body(
    got_ref, choice_hbm, aux_hbm, ops_hbm, _, dep_ref, out_ref, choice_ref, aux_ref, ops_ref, sems
):
    size = GROUP * BLK
    parts = [pl.ds(first, size) for first in range(0, ALL_OBS * BLK, size)]
    pairs = [(choice_hbm, choice_ref), (aux_hbm, aux_ref)]
    waits = copies(sems, *pairs, *[(ops_hbm.at[part], ops_ref.at[part]) for part in parts])
    waits[0].wait()
    base = PARTS * SENT
    pick = jnp.concatenate([choice_ref[base + half * ALL_OBS : base + (half + 1) * ALL_OBS, :] for half in range(2)], axis=1)
    seen = jnp.dot(pick, got_ref[...], preferred_element_type=F32).astype(BF16)
    waits[1].wait()
    line = iota((GROUP, BLK), 0)
    scaled = []
    for at in range(ALL_OBS // GROUP):
        waits[2 + at].wait()
        first = at * GROUP
        rows = slice(first, first + GROUP)
        product = jnp.zeros((GROUP, BLK), F32)
        for i in range(GROUP):
            one = lax.dot_general(
                seen[rows],
                ops_ref[(first + i) * BLK : (first + i + 1) * BLK, :],
                (((1,), (1,)), ((), ())),
                preferred_element_type=F32,
            )
            product = jnp.where(line == i, one, product)
        departure = product - aux_ref[first : first + GROUP, :]
        dep_ref[rows, :] = departure
        weight = aux_ref[ALL_OBS + first : ALL_OBS + first + GROUP, :]
        scaled.append((weight * departure).astype(BF16))
    steps = []
    for at, block in enumerate(scaled):
        first = at * GROUP
        steps.append(
            jnp.dot(
                spread_out(block), ops_ref[first * BLK : (first + GROUP) * BLK, :], preferred_element_type=F32
            ).astype(BF16)
        )
    increments = jnp.concatenate(steps, axis=0)
    out_ref[...] = jnp.dot(choice_ref[:base, :ALL_OBS], increments, preferred_element_type=F32).astype(BF16)


PAIRS = ((2, 3), (0, 1))
SIDES = ((0, 0, 0, BLOCKS), (1, BLOCKS, HALF * LEV, HALF * LEV), (2, BLOCKS + HALF * LEV, 0, HALF * LEV))


def prepare_body(asked_ref, lam_ref, south_ref, north_ref, dep_ref, put_ref, y_ref, out_ref):
    out_ref[...] = dep_ref[...]
    asked = jnp.transpose(asked_ref[...].astype(F32))
    for at, steps in enumerate(PAIRS):
        for side, base, start, size in SIDES:
            named = jnp.concatenate(
                [asked[side * SLOTS + 2 * step + nth :][:1] for step in steps for nth in range(2)], axis=1
            )
            line = (iota((size, 4 * PARTS), 0) + start).astype(F32)
            put_ref[at, base : base + size, :] = jnp.where(line == named, 1.0, 0.0).astype(BF16)
    for block_ref, first, rows in ((south_ref, 0, HALO), (lam_ref, HALO, ROWS), (north_ref, HALO + ROWS, HALO)):
        for row in range(0, rows, 2):
            both = block_ref[pl.ds(row * LEV, 2 * LEV), :].astype(F32)
            for i in range(2):
                y_ref[first + row + i] = -widen(both[i * LEV : (i + 1) * LEV])


def adjoint_body(got_ref, put_ref, first_ref, misfit_ref, coef_ref, out_ref, got_f, flat_ref, a_ref, y_ref, tmp_ref):
    got_f[...] = got_ref[...].astype(F32)
    for at, steps in enumerate(PAIRS):
        for side, base, start, size in SIDES:
            sides = []
            for i, step in enumerate(steps):
                terms = jnp.concatenate(
                    [got_f[pl.ds(side * SLOTS + 2 * step + nth, PARTS, stride=SENT), :] for nth in range(2)], axis=0
                ).astype(BF16)
                zero = jnp.zeros_like(terms)
                sides.append(jnp.concatenate([terms, zero] if i == 0 else [zero, terms], axis=0))
            added = jnp.dot(
                put_ref[at, base : base + size, :], jnp.concatenate(sides, axis=1), preferred_element_type=F32
            )
            flat = (1, 0, 3)[side]
            for i, step in enumerate(steps):
                for tile in range(size // LEV):
                    half, run = tile // HALF, tile % HALF
                    flat_ref[step * 4 + flat + half, :, run * BLK : (run + 1) * BLK] = added[
                        tile * LEV : (tile + 1) * LEV, i * BLK : (i + 1) * BLK
                    ]
    for step in range(STEPS - 1, -1, -1):
        edge = STEPS - 1 - step
        before = first_ref if edge == 0 else y_ref
        for row in range(edge, EXT - edge):
            part = row % 4
            a_ref[row] = before[row] + widen(flat_ref[step * 4 + row // 4, :, part * LON : (part + 1) * LON])
        for row in range(edge + 1, EXT - edge - 1):
            v = a_ref[row]
            pulled = (
                row_of(coef_ref, 0, row) * v
                + pltpu.roll(row_of(coef_ref, 1, row) * v, 1, 1)
                + pltpu.roll(row_of(coef_ref, 2, row) * v, WIDE - 1, 1)
                + row_of(coef_ref, 3, row - 1) * a_ref[row - 1]
                + row_of(coef_ref, 4, row + 1) * a_ref[row + 1]
            )
            if step:
                y_ref[row] = pulled
            else:
                put_row(tmp_ref, row - HALO, pulled)
    out_ref[...] = gathered(tmp_ref) + misfit_ref[...]


def shape(dims, dtype):
    return jax.ShapeDtypeStruct(dims, dtype)


def exchange(block):
    return lax.all_to_all(block, "space", split_axis=0, concat_axis=0, tiled=True)


def local(
    increments,
    background,
    error_weight,
    neighbor_weights,
    operators,
    values,
    obs_weight,
    owners,
    columns,
):
    fields = LEV * ROWS
    start = increments.reshape(fields, LON)
    owner = owners.reshape(STEPS, 1, OBS)
    windows, parts = lax.axis_size("tm"), lax.axis_size("space")
    vmem = pl.BlockSpec(memory_space=pltpu.VMEM)
    home = pl.BlockSpec(memory_space=pltpu.HBM)
    anywhere = pl.BlockSpec(memory_space=pl.ANY)
    sems = pltpu.SemaphoreType.DMA
    field = pltpu.VMEM((fields, LON), F32)
    weights = pltpu.VMEM((4, ROWS, LON), F32)
    runs = pltpu.VMEM((WIDE // BLK, fields, BLK), F32)
    wide = pltpu.VMEM((EXT, LEV, WIDE), F32)

    request, choice = pl.pallas_call(
        request_body,
        in_specs=[home, home],
        out_shape=(
            shape((PARTS, BLK), I32),
            shape((PARTS * SENT + 2 * ALL_OBS, BLK), BF16),
        ),
        scratch_shapes=[pltpu.VMEM((STEPS, 1, OBS), I32), pltpu.VMEM((STEPS, OBS), I32), sems((2,))],
        name="request",
        compiler_params=params(60),
    )(owner, columns.reshape(STEPS, OBS))
    asked = exchange(request)

    edge = shape((HALO * LEV + 4 * HALO, LON), BF16)
    low, high, aux = pl.pallas_call(
        edges_body,
        in_specs=[home, home, home, home, anywhere],
        out_shape=(edge, edge, shape((2 * ALL_OBS, BLK), F32)),
        scratch_shapes=[runs, field, weights, sems((4,))],
        name="edges",
        compiler_params=params(60),
    )(start, neighbor_weights, values.reshape(ALL_OBS, BLK), obs_weight.reshape(ALL_OBS, BLK), request)
    south = lax.ppermute(high, "space", [(i, i + 1) for i in range(parts - 1)])
    north = lax.ppermute(low, "space", [(i + 1, i) for i in range(parts - 1)])

    edge_f = pltpu.VMEM((HALO * LEV + 4 * HALO, LON), F32)
    tables, last, coeffs = pl.pallas_call(
        forward_body,
        in_specs=[home, home, vmem, vmem],
        out_shape=(
            shape((STEPS, BLOCKS, BLK), BF16),
            shape((fields, LON), BF16),
            shape((5, EXT, WIDE), F32),
        ),
        scratch_shapes=[
            pltpu.VMEM((2 * EXT, LEV, WIDE), F32),
            pltpu.VMEM((2, LEV, HALF * BLK), F32),
            edge_f,
            edge_f,
            runs,
            field,
            weights,
            sems((2,)),
        ],
        name="forward",
        compiler_params=params(20),
    )(start, neighbor_weights, south, north)

    blocks, last = pl.pallas_call(
        gather_body,
        in_specs=[vmem, vmem, anywhere],
        out_specs=(vmem, anywhere),
        out_shape=(shape((PARTS * SLOTS, BLK), BF16), shape((fields, LON), BF16)),
        input_output_aliases={2: 1},
        scratch_shapes=[pltpu.VMEM((PARTS * SLOTS, BLK), F32)],
        name="gather",
        compiler_params=params(16),
    )(asked, tables, last)
    got = exchange(blocks)

    previous = lax.ppermute(last, "tm", [(i, i + 1) for i in range(windows - 1)])
    first = (lax.axis_index("tm") == 0).astype(I32).reshape(1)
    side = shape((HALO * LEV, LON), BF16)
    misfit, sent, sent_low, sent_high, token = pl.pallas_call(
        misfit_body,
        in_specs=[pl.BlockSpec(memory_space=pltpu.SMEM), home, home, home, vmem],
        out_shape=(shape((fields, LON), F32), shape((fields, LON), BF16), side, side, shape((8, BLK), F32)),
        scratch_shapes=[runs, field, field, field, sems((3,))],
        name="misfit",
        compiler_params=params(16),
    )(first, start, error_weight.reshape(fields, LON), background.reshape(fields, LON), previous)

    def back(block, shift):
        route = []
        for k in range(1, windows):
            for p in range(parts):
                if 0 <= p + shift < parts:
                    route.append((k * parts + p, (k - 1) * parts + p + shift))
        return lax.ppermute(block, ("tm", "space"), route)

    lam = back(sent, 0)
    lam_south = back(sent_high, 1)
    lam_north = back(sent_low, -1)

    per_obs = shape((ALL_OBS, BLK), F32)
    found, slots = pl.pallas_call(
        observe_body,
        in_specs=[vmem] + [home] * 3 + [anywhere],
        out_shape=(per_obs, shape((PARTS * SENT, BLK), BF16)),
        scratch_shapes=[
            pltpu.VMEM((PARTS * SENT + 2 * ALL_OBS, BLK), BF16),
            pltpu.VMEM((2 * ALL_OBS, BLK), F32),
            pltpu.VMEM((ALL_OBS * BLK, BLK), BF16),
            sems((2 + ALL_OBS // GROUP,)),
        ],
        name="observe",
        compiler_params=params(53.75),
    )(
        got,
        choice,
        aux,
        operators.reshape(ALL_OBS * BLK, BLK),
        token,
    )
    arrived = exchange(slots)

    put, ahead, departures = pl.pallas_call(
        prepare_body,
        out_shape=(shape((2, 2 * BLOCKS, BLK), BF16), shape((EXT, LEV, WIDE), F32), per_obs),
        name="prepare",
        compiler_params=params(16),
    )(asked, lam, lam_south, lam_north, found)

    gradient = pl.pallas_call(
        adjoint_body,
        out_shape=shape((fields, LON), F32),
        scratch_shapes=[
            pltpu.VMEM((PARTS * SENT, BLK), F32),
            pltpu.VMEM((4 * STEPS, LEV, HALF * BLK), F32),
            wide,
            wide,
            runs,
        ],
        name="adjoint",
        compiler_params=params(20),
    )(arrived, put, ahead, misfit, coeffs)
    return (gradient.reshape(increments.shape), departures.reshape(values.shape))


def solution(mesh):
    in_specs = (
        P("tm", None, "space", None),
        P(None, "space", None),
        P(None, "space", None),
        P(None, "space", None),
        P("tm", None, "space", None, None),
        P("tm", None, "space", None),
        P("tm", None, "space", None),
        P("tm", None, "space", None),
        P("tm", None, "space"),
    )
    out_specs = (P("tm", None, "space", None), P("tm", None, "space", None))
    return jax.shard_map(local, mesh=mesh, in_specs=in_specs, out_specs=out_specs, check_vma=False)
```

time: 265 us -> 81 us (0.31)
  the two profiles are of different devices: /device:TPU:286 before, /device:TPU:223 now
where the time goes in v1:
time: 81 us; the launch traced here: 80.3 us
  starting transfers between devices  46.2 us (57%)
  Pallas kernels  17.8 us (22%)
  waiting for transfers between devices  10.6 us (13%)
  local copies, waits for them, and re-layouts  4.9 us (6%)
    all_to_all x3, starting transfers between devices, exchange(): lax.all_to_all(block, 'space', split_axis=0, concat_axis=0, tiled=True)  26.5 us
    ppermute x3, waiting for transfers between devices, back(): return lax.ppermute(block, ('tm', 'space'), route)  9.44 us
    ppermute x1, starting transfers between devices, local(): lax.ppermute(last, 'tm', [(i, i + 1) for i in range(windows - 1)])  6.88 us
    ppermute x3, starting transfers between devices, back(): return lax.ppermute(block, ('tm', 'space'), route)  6.57 us
    unnamed x10, local copies, waits for them, and re-layouts  4.9 us
    pallas_call x1, Pallas kernels, local(): pl.pallas_call(observe_body, in_specs=[vmem] + [home] * 3 + [anywhere], o...  4.89 us
    ppermute x1, starting transfers between devices, local(): south = lax.ppermute(high, 'space', [(i, i + 1) for i in range(parts - 1)])  4.33 us
    pallas_call x1, Pallas kernels, local(): pl.pallas_call(forward_body, in_specs=[home, home, vmem, vmem], out_shape...  3.59 us
  transfers between devices with their start and end apart: 9, of which 3 were waited for; matrix products, arithmetic and copies ran while one was open for 0% of the time, Pallas kernels for 7%

profile of v1, /device:TPU:223, one launch (start us, length us, event | category | flops | bytes accessed | tf_op | source)
XLA Modules:
  0.0 80.3 jit_solution(11014718908769351289)
XLA Ops:
  0.6 1.7 %request.1 = (s32[32,128]{1,0:T(8,128)}, bf16[960,128]{1,0:T(8,128)(2,1)}) custom-call(s32[4,1,24]{2,1,0:T(1,128)} %bitcast.36, s32[4,24]{1,0:T(4,128)} %bitcast.37), custom_call_target="tpu_custom_call" | custom-call | tf_op jit(solution)/shard_map/request/pallas_call | solution.py:382
  2.4 2.0 %edges.1 = (bf16[48,1440]{1,0:T(8,128)(2,1)}, bf16[48,1440]{1,0:T(8,128)(2,1)}, f32[192,128]{1,0:T(8,128)}) custom-call(f32[64,1440]{1,0:T(8,128)} %bitcast.21, f32[4,8,1440]{2,1,0:T(8,128)} %wts_hbm.3, f32[96,128]{1,0:T(8,128)} %bitcast.34, f32[96,128]{1,0:T(8,128)} %bitcast.35, s32[32,128]{1,0:T(8,128)} %get-tuple-element.22._), custom_call_target="tpu_custom_call" | custom-call | tf_op jit(solution)/shard_map/edges/pallas_call | solution.py:396
  4.3 4.3 %collective-permute-start = (bf16[48,1440]{1,0:T(8,128)(2,1)}, bf16[48,1440]{1,0:T(8,128)(2,1)S(1)}, u32[]{:S(2)}, u32[]{:S(2)}) collective-permute-start(bf16[48,1440]{1,0:T(8,128)(2,1)} %get-tuple-element.23), channel_id=1, source_target_pairs={{0,1},{1,2},{2,3},{3,4},{4,5},{5,6},{6,7},{7,8},{8,9},{9,10},{10,1... | collective-permute-start | bytes 414728 | tf_op jit(solution)/shard_map/ppermute | solution.py:404
  8.7 1.9 %collective-permute-start.1 = (bf16[48,1440]{1,0:T(8,128)(2,1)}, bf16[48,1440]{1,0:T(8,128)(2,1)S(1)}, u32[]{:S(2)}, u32[]{:S(2)}) collective-permute-start(bf16[48,1440]{1,0:T(8,128)(2,1)} %get-tuple-element.24), channel_id=1, source_target_pairs={{1,0},{2,1},{3,2},{4,3},{5,4},{6,5},{7,6},{8,7},{9,8},{10,9},{11,1... | collective-permute-start | bytes 414728 | tf_op jit(solution)/shard_map/ppermute | solution.py:405
  10.6 9.2 %all-to-all-start = ((s32[32,1,128]{2,1,0:T(1,128)}), s32[32,1,128]{2,1,0:T(1,128)S(1)}, u32[]{:S(2)}, u32[]{:S(2)}) async-start(s32[32,1,128]{2,1,0:T(1,128)} %bitcast.33), calls=%async_computation | async-start | bytes 32768 | tf_op jit(solution)/shard_map/all_to_all | solution.py:355
  19.8 0.0 collective-permute-done.south_ref
  19.8 0.0 collective-permute-done.1.north_ref
  19.8 0.0 copy-start
  19.8 1.0 %copy-done = f32[1,8,8,1440]{3,2,1,0:T(8,128)S(1)} copy-done((f32[1,8,8,1440]{3,2,1,0:T(8,128)S(1)}, f32[1,8,8,1440]{3,2,1,0:T(8,128)}, u32[]{:S(2)}) %copy-start) | copy-done | bytes 368664
  20.8 0.9 %copy-done.2 = f32[4,8,1440]{2,1,0:T(8,128)S(1)} copy-done((f32[4,8,1440]{2,1,0:T(8,128)S(1)}, f32[4,8,1440]{2,1,0:T(8,128)}, u32[]{:S(2)}) %copy-start.2) | copy-done | bytes 184344
  21.7 3.6 %forward.1 = (bf16[4,720,128]{2,1,0:T(8,128)(2,1)S(1)}, bf16[64,1440]{1,0:T(8,128)(2,1)S(1)}, f32[5,16,1536]{2,1,0:T(8,128)S(1)}) custom-call(f32[64,1440]{1,0:T(8,128)S(1)} %bitcast.22, f32[4,8,1440]{2,1,0:T(8,128)S(1)} %copy-done.2, bf16[48,1440]{1,0:T(8,128)(2,1)S(1)} %collective-permute-done.south_ref, bf16[48,1440]{1,0:T(8,128)(2,1)S(1)} %collective-permute-done.1.north_ref), custom_call_target="tpu_custom_call" | custom-call | tf_op jit(solution)/shard_map/forward/pallas_call | solution.py:408
  25.3 0.0 all-to-all-done
  25.3 1.0 %gather.1 = (bf16[256,128]{1,0:T(8,128)(2,1)}, bf16[64,1440]{1,0:T(8,128)(2,1)S(1)}) custom-call(s32[32,128]{1,0:T(8,128)S(1)} %bitcast.28, bf16[4,720,128]{2,1,0:T(8,128)(2,1)S(1)} %get-tuple-element.25.table_ref, bf16[64,1440]{1,0:T(8,128)(2,1)S(1)} %get-tuple-element.26._), custom_call_target="tpu_custom_call", output_to_operand_aliasing={{1}: (2, {})} | custom-call | tf_op jit(solution)/shard_map/gather/pallas_call | solution.py:430
  26.3 6.9 %collective-permute-start.2 = (bf16[64,1440]{1,0:T(8,128)(2,1)S(1)}, bf16[64,1440]{1,0:T(8,128)(2,1)S(1)}, u32[]{:S(2)}, u32[]{:S(2)}) collective-permute-start(bf16[64,1440]{1,0:T(8,128)(2,1)S(1)} %get-tuple-element.30), channel_id=1, source_target_pairs={{0,32},{32,64},{64,96},{96,128},{128,160},{160,192},{192,224},{224... | collective-permute-start | bytes 552968 | tf_op jit(solution)/shard_map/ppermute | solution.py:442
  33.2 9.2 %all-to-all-start.1 = ((bf16[32,8,128]{2,1,0:T(8,128)(2,1)}), bf16[32,8,128]{2,1,0:T(8,128)(2,1)S(1)}, u32[]{:S(2)}, u32[]{:S(2)}) async-start(bf16[32,8,128]{2,1,0:T(8,128)(2,1)} %bitcast.9), calls=%async_computation.1 | async-start | bytes 131072 | tf_op jit(solution)/shard_map/all_to_all | solution.py:355
  42.4 0.0 collective-permute-done.2.prev_ref
  42.4 0.0 copy-start.1
  42.5 1.0 %copy-done.1 = f32[1,8,8,1440]{3,2,1,0:T(8,128)S(1)} copy-done((f32[1,8,8,1440]{3,2,1,0:T(8,128)S(1)}, f32[1,8,8,1440]{3,2,1,0:T(8,128)}, u32[]{:S(2)}) %copy-start.1) | copy-done | bytes 368664
  43.4 1.0 %copy-done.3 = f32[8,8,1440]{2,1,0:T(8,128)S(1)} copy-done((f32[8,8,1440]{2,1,0:T(8,128)S(1)}, f32[8,8,1440]{2,1,0:T(8,128)}, u32[]{:S(2)}) %copy-start.3) | copy-done | bytes 368664
  44.4 1.0 %copy-done.4 = f32[8,8,1440]{2,1,0:T(8,128)S(1)} copy-done((f32[8,8,1440]{2,1,0:T(8,128)S(1)}, f32[8,8,1440]{2,1,0:T(8,128)}, u32[]{:S(2)}) %copy-start.4) | copy-done | bytes 368664
  45.4 0.8 %misfit.1 = (f32[64,1440]{1,0:T(8,128)S(1)}, bf16[64,1440]{1,0:T(8,128)(2,1)S(1)}, bf16[32,1440]{1,0:T(8,128)(2,1)S(1)}, bf16[32,1440]{1,0:T(8,128)(2,1)S(1)}, f32[8,128]{1,0:T(8,128)S(1)}) custom-call(s32[1]{0:T(128)} %bitcast.12.first_ref, f32[64,1440]{1,0:T(8,128)S(1)} %bitcast.23, f32[64,1440]{1,0:T(8,128)S(1)} %bitcast.25, f32[64,1440]{1,0:T(8,128)S(1)} %bitcast.26, ...), custom_call_target="tpu_custom_call" | custom-call | tf_op jit(solution)/shard_map/misfit/pallas_call | solution.py:445
  46.3 1.2 %all-to-all-done.1 = bf16[32,8,128]{2,1,0:T(8,128)(2,1)S(1)} async-done(((bf16[32,8,128]{2,1,0:T(8,128)(2,1)}), bf16[32,8,128]{2,1,0:T(8,128)(2,1)S(1)}, u32[]{:S(2)}, u32[]{:S(2)}) %all-to-all-start.1) | async-done | bytes 65568 | tf_op jit(solution)/shard_map/all_to_all | solution.py:355
  47.4 4.9 %observe.1 = (f32[96,128]{1,0:T(8,128)S(1)}, bf16[768,128]{1,0:T(8,128)(2,1)}) custom-call(bf16[256,128]{1,0:T(8,128)(2,1)S(1)} %bitcast.27, bf16[960,128]{1,0:T(8,128)(2,1)} %get-tuple-element.28.choice_hbm, f32[192,128]{1,0:T(8,128)} %get-tuple-element.29.aux_hbm, bf16[12288,128]{1,0:T(8,128)(2,1)} %bitcast.30, f32[8,128]{1,0:T(8,128)S(1)} %get-tuple-element.31._), custom_call_target="tpu_custom_call" | custom-call | tf_op jit(solution)/shard_map/observe/pallas_call | solution.py:467
  52.3 8.1 %all-to-all-start.2 = ((bf16[32,24,128]{2,1,0:T(8,128)(2,1)}), bf16[32,24,128]{2,1,0:T(8,128)(2,1)S(1)}, u32[]{:S(2)}, u32[]{:S(2)}) async-start(bf16[32,24,128]{2,1,0:T(8,128)(2,1)} %bitcast.32), calls=%async_computation.2 | async-start | bytes 393216 | tf_op jit(solution)/shard_map/all_to_all | solution.py:355
  60.4 1.9 %collective-permute-start.3 = (bf16[64,1440]{1,0:T(8,128)(2,1)S(1)}, bf16[64,1440]{1,0:T(8,128)(2,1)S(1)}, u32[]{:S(2)}, u32[]{:S(2)}) collective-permute-start(bf16[64,1440]{1,0:T(8,128)(2,1)S(1)} %get-tuple-element.33), channel_id=1, source_target_pairs={{32,0},{33,1},{34,2},{35,3},{36,4},{37,5},{38,6},{39,7},{40,8},{41... | collective-permute-start | bytes 552968 | tf_op jit(solution)/shard_map/ppermute | solution.py:460
  62.4 2.7 %collective-permute-start.4 = (bf16[32,1440]{1,0:T(8,128)(2,1)S(1)}, bf16[32,1440]{1,0:T(8,128)(2,1)S(1)}, u32[]{:S(2)}, u32[]{:S(2)}) collective-permute-start(bf16[32,1440]{1,0:T(8,128)(2,1)S(1)} %get-tuple-element.34), channel_id=1, source_target_pairs={{32,1},{33,2},{34,3},{35,4},{36,5},{37,6},{38,7},{39,8},{40,9},{41... | collective-permute-start | bytes 276488 | tf_op jit(solution)/shard_map/ppermute | solution.py:460
  65.1 1.9 %collective-permute-start.5 = (bf16[32,1440]{1,0:T(8,128)(2,1)S(1)}, bf16[32,1440]{1,0:T(8,128)(2,1)S(1)}, u32[]{:S(2)}, u32[]{:S(2)}) collective-permute-start(bf16[32,1440]{1,0:T(8,128)(2,1)S(1)} %get-tuple-element.35), channel_id=1, source_target_pairs={{33,0},{34,1},{35,2},{36,3},{37,4},{38,5},{39,6},{40,7},{41,8},{42... | collective-permute-start | bytes 276488 | tf_op jit(solution)/shard_map/ppermute | solution.py:460
  67.0 3.4 %collective-permute-done.4.south_ref = bf16[32,1440]{1,0:T(8,128)(2,1)S(1)} collective-permute-done((bf16[32,1440]{1,0:T(8,128)(2,1)S(1)}, bf16[32,1440]{1,0:T(8,128)(2,1)S(1)}, u32[]{:S(2)}, u32[]{:S(2)}) %collective-permute-start.4) | collective-permute-done | bytes 92192 | tf_op jit(solution)/shard_map/ppermute | solution.py:460
  70.4 6.1 %collective-permute-done.5.north_ref = bf16[32,1440]{1,0:T(8,128)(2,1)S(1)} collective-permute-done((bf16[32,1440]{1,0:T(8,128)(2,1)S(1)}, bf16[32,1440]{1,0:T(8,128)(2,1)S(1)}, u32[]{:S(2)}, u32[]{:S(2)}) %collective-permute-start.5) | collective-permute-done | bytes 92192 | tf_op jit(solution)/shard_map/ppermute | solution.py:460
  76.5 0.0 collective-permute-done.3.lam_ref
  76.5 0.8 %prepare.1 = (bf16[2,1440,128]{2,1,0:T(8,128)(2,1)S(1)}, f32[16,8,1536]{2,1,0:T(8,128)S(1)}, f32[96,128]{1,0:T(8,128)}) custom-call(s32[32,128]{1,0:T(8,128)S(1)} %bitcast.29, bf16[64,1440]{1,0:T(8,128)(2,1)S(1)} %collective-permute-done.3.lam_ref, bf16[32,1440]{1,0:T(8,128)(2,1)S(1)} %collective-permute-done.4.south_ref, ...), custom_call_target="tpu_custom_call" | custom-call | tf_op jit(solution)/shard_map/prepare/pallas_call | solution.py:488
  77.3 3.0 %adjoint.1 = f32[64,1440]{1,0:T(8,128)} custom-call(bf16[768,128]{1,0:T(8,128)(2,1)S(1)} %bitcast.24, bf16[2,1440,128]{2,1,0:T(8,128)(2,1)S(1)} %get-tuple-element.37.put_ref, f32[16,8,1536]{2,1,0:T(8,128)S(1)} %get-tuple-element.38.first_ref, f32[64,1440]{1,0:T(8,128)S(1)} %get-tuple-element.39.misfit_ref, f32[5,16,1536]{2,1,0:T(8,128)S(1)} %get-tuple-element.40.coef_ref), custom_call_target="tpu_custom_call" | custom-call | tf_op jit(solution)/shard_map/adjoint/pallas_call | solution.py:495
  (4 shorter events, 0.0 us)
Async XLA Ops:
  4.3 15.5 %collective-permute-start = (bf16[48,1440]{1,0:T(8,128)(2,1)}, bf16[48,1440]{1,0:T(8,128)(2,1)S(1)}, u32[]{:S(2)}, u32[]{:S(2)}) collective-permute-start(bf16[48,1440]{1,0:T(8,128)(2,1)} %get-tuple-element.23), channel_id=1, source_target_pairs={{0,1},{1,2},{2,3},{3,4},{4,5},{5,6},{6,7},{7,8},{8,9},{9,10},{10,1... | collective-permute-start | bytes 414728 | tf_op jit(solution)/shard_map/ppermute | solution.py:404
  8.7 11.2 %collective-permute-start.1 = (bf16[48,1440]{1,0:T(8,128)(2,1)}, bf16[48,1440]{1,0:T(8,128)(2,1)S(1)}, u32[]{:S(2)}, u32[]{:S(2)}) collective-permute-start(bf16[48,1440]{1,0:T(8,128)(2,1)} %get-tuple-element.24), channel_id=1, source_target_pairs={{1,0},{2,1},{3,2},{4,3},{5,4},{6,5},{7,6},{8,7},{9,8},{10,9},{11,1... | collective-permute-start | bytes 414728 | tf_op jit(solution)/shard_map/ppermute | solution.py:405
  10.6 14.8 %all-to-all-start = ((s32[32,1,128]{2,1,0:T(1,128)}), s32[32,1,128]{2,1,0:T(1,128)S(1)}, u32[]{:S(2)}, u32[]{:S(2)}) async-start(s32[32,1,128]{2,1,0:T(1,128)} %bitcast.33), calls=%async_computation | async-start | bytes 32768 | tf_op jit(solution)/shard_map/all_to_all | solution.py:355
  19.8 1.0 %copy-start = (f32[1,8,8,1440]{3,2,1,0:T(8,128)S(1)}, f32[1,8,8,1440]{3,2,1,0:T(8,128)}, u32[]{:S(2)}) copy-start(f32[1,8,8,1440]{3,2,1,0:T(8,128)} %param.9) | copy-start | bytes 1105924
  20.8 0.9 %copy-start.2 = (f32[4,8,1440]{2,1,0:T(8,128)S(1)}, f32[4,8,1440]{2,1,0:T(8,128)}, u32[]{:S(2)}) copy-start(f32[4,8,1440]{2,1,0:T(8,128)} %wts_hbm.3) | copy-start | bytes 552964
  26.3 16.1 %collective-permute-start.2 = (bf16[64,1440]{1,0:T(8,128)(2,1)S(1)}, bf16[64,1440]{1,0:T(8,128)(2,1)S(1)}, u32[]{:S(2)}, u32[]{:S(2)}) collective-permute-start(bf16[64,1440]{1,0:T(8,128)(2,1)S(1)} %get-tuple-element.30), channel_id=1, source_target_pairs={{0,32},{32,64},{64,96},{96,128},{128,160},{160,192},{192,224},{224... | collective-permute-start | bytes 552968 | tf_op jit(solution)/shard_map/ppermute | solution.py:442
  33.2 14.2 %all-to-all-start.1 = ((bf16[32,8,128]{2,1,0:T(8,128)(2,1)}), bf16[32,8,128]{2,1,0:T(8,128)(2,1)S(1)}, u32[]{:S(2)}, u32[]{:S(2)}) async-start(bf16[32,8,128]{2,1,0:T(8,128)(2,1)} %bitcast.9), calls=%async_computation.1 | async-start | bytes 131072 | tf_op jit(solution)/shard_map/all_to_all | solution.py:355
  42.4 1.0 %copy-start.1 = (f32[1,8,8,1440]{3,2,1,0:T(8,128)S(1)}, f32[1,8,8,1440]{3,2,1,0:T(8,128)}, u32[]{:S(2)}) copy-start(f32[1,8,8,1440]{3,2,1,0:T(8,128)} %param.9) | copy-start | bytes 1105924
  43.4 1.0 %copy-start.3 = (f32[8,8,1440]{2,1,0:T(8,128)S(1)}, f32[8,8,1440]{2,1,0:T(8,128)}, u32[]{:S(2)}) copy-start(f32[8,8,1440]{2,1,0:T(8,128)} %param.11) | copy-start | bytes 1105924
  44.4 1.0 %copy-start.4 = (f32[8,8,1440]{2,1,0:T(8,128)S(1)}, f32[8,8,1440]{2,1,0:T(8,128)}, u32[]{:S(2)}) copy-start(f32[8,8,1440]{2,1,0:T(8,128)} %param.10) | copy-start | bytes 1105924
  52.3 25.0 %all-to-all-start.2 = ((bf16[32,24,128]{2,1,0:T(8,128)(2,1)}), bf16[32,24,128]{2,1,0:T(8,128)(2,1)S(1)}, u32[]{:S(2)}, u32[]{:S(2)}) async-start(bf16[32,24,128]{2,1,0:T(8,128)(2,1)} %bitcast.32), calls=%async_computation.2 | async-start | bytes 393216 | tf_op jit(solution)/shard_map/all_to_all | solution.py:355
  60.4 16.0 %collective-permute-start.3 = (bf16[64,1440]{1,0:T(8,128)(2,1)S(1)}, bf16[64,1440]{1,0:T(8,128)(2,1)S(1)}, u32[]{:S(2)}, u32[]{:S(2)}) collective-permute-start(bf16[64,1440]{1,0:T(8,128)(2,1)S(1)} %get-tuple-element.33), channel_id=1, source_target_pairs={{32,0},{33,1},{34,2},{35,3},{36,4},{37,5},{38,6},{39,7},{40,8},{41... | collective-permute-start | bytes 552968 | tf_op jit(solution)/shard_map/ppermute | solution.py:460
  62.4 8.0 %collective-permute-start.4 = (bf16[32,1440]{1,0:T(8,128)(2,1)S(1)}, bf16[32,1440]{1,0:T(8,128)(2,1)S(1)}, u32[]{:S(2)}, u32[]{:S(2)}) collective-permute-start(bf16[32,1440]{1,0:T(8,128)(2,1)S(1)} %get-tuple-element.34), channel_id=1, source_target_pairs={{32,1},{33,2},{34,3},{35,4},{36,5},{37,6},{38,7},{39,8},{40,9},{41... | collective-permute-start | bytes 276488 | tf_op jit(solution)/shard_map/ppermute | solution.py:460
  65.1 11.4 %collective-permute-start.5 = (bf16[32,1440]{1,0:T(8,128)(2,1)S(1)}, bf16[32,1440]{1,0:T(8,128)(2,1)S(1)}, u32[]{:S(2)}, u32[]{:S(2)}) collective-permute-start(bf16[32,1440]{1,0:T(8,128)(2,1)S(1)} %get-tuple-element.35), channel_id=1, source_target_pairs={{33,0},{34,1},{35,2},{36,3},{37,4},{38,5},{39,6},{40,7},{41,8},{42... | collective-permute-start | bytes 276488 | tf_op jit(solution)/shard_map/ppermute | solution.py:460

commit v2 on v1

v2 whole, which is shorter than its diff:
```python
import jax
import jax.numpy as jnp
from jax import lax
from jax.experimental import pallas as pl
from jax.experimental.pallas import tpu as pltpu
from jax.sharding import PartitionSpec as P

LEV = 8
ROWS = 8
LON = 1440
WIDE = 1536
PAD = 48
STEPS = 4
HALO = 4
EXT = ROWS + 2 * HALO
FULL = 3 * ROWS
FIELD = LEV * ROWS
SENT_ROWS = FIELD + 4 * ROWS + FIELD
OBS = 24
ALL_OBS = STEPS * OBS
BLK = 128
PARTS = 32
SLOTS = 2 * STEPS
SENT = 3 * SLOTS
HALF = 45
BLOCKS = 2 * HALF * LEV
F32 = jnp.float32
BF16 = jnp.bfloat16
I32 = jnp.int32


def iota(shape, dim):
    return lax.broadcasted_iota(I32, shape, dim)


def params(mib):
    return pltpu.CompilerParams(vmem_limit_bytes=int(mib * (1 << 20)))


def copies(sems, *pairs):
    found = [pltpu.make_async_copy(src, dst, sems.at[i]) for i, (src, dst) in enumerate(pairs)]
    for copy in found:
        copy.start()
    return found


def owner_rank(own_ref, step):
    sub, lane = iota((OBS, OBS), 0), iota((OBS, OBS), 1)
    across = jnp.broadcast_to(own_ref[step], (OBS, OBS)).astype(F32)
    down = jnp.sum(jnp.where(sub == lane, across, 0.0), axis=1, keepdims=True)
    same = down == across
    rank_across = jnp.sum(jnp.where(same & (sub < lane), 1.0, 0.0), axis=0, keepdims=True)
    rank_down = jnp.sum(jnp.where(same & (lane < sub), 1.0, 0.0), axis=1, keepdims=True)
    return down, across[:1], rank_down, rank_across


def request_body(own_hbm, col_hbm, _, out_ref, choice_ref, own_ref, col_ref, sems):
    for copy in copies(sems, (own_hbm, own_ref), (col_hbm, col_ref)):
        copy.wait()
    dest = iota((PARTS, OBS), 0).astype(F32)
    lane = iota((PARTS, BLK), 1)
    line = iota((PARTS, BLK), 0)
    from_lane = iota((OBS, PARTS * SLOTS), 1).astype(F32)
    asked = jnp.zeros((PARTS, BLK), F32)
    sends = [[], [], []]
    picks = []
    for step in range(STEPS):
        down, across, rank_down, rank_across = owner_rank(own_ref, step)
        block = col_ref[pl.ds(step, 1), :]
        group = (block * 1457) >> 16
        row = ((group & 1) * HALF + block - HALF * group) * LEV + (group >> 1)
        value = (row + 1).astype(F32)
        for nth in range(2):
            hit = (across == dest) & (rank_across == float(nth))
            found = jnp.sum(jnp.where(hit, value, 0.0), axis=1, keepdims=True)
            asked = jnp.where(lane == 2 * step + nth, found, asked)
        picks.append(jnp.where(from_lane == down * SLOTS + (2.0 * step) + rank_down, 1.0, 0.0))
        for side, shift in enumerate((0.0, 1.0, -1.0)):
            sends[side].append((across + shift) * SENT + (side * SLOTS + 2.0 * step) + rank_across)
    below = jnp.where(line == 0, 0.0, pltpu.roll(asked, 1, 0))
    above = jnp.where(line == PARTS - 1, 0.0, pltpu.roll(asked, PARTS - 1, 0))
    asked = asked + pltpu.roll(below, SLOTS, 1) + pltpu.roll(above, 2 * SLOTS, 1)
    out_ref[...] = asked.astype(I32) - 1
    pick = jnp.concatenate(picks, axis=0).astype(BF16)
    for half in range(2):
        choice_ref[pl.ds(PARTS * SENT + half * ALL_OBS, ALL_OBS), :] = pick[:, half * BLK : (half + 1) * BLK]
    spare = jnp.full((1, BLK - ALL_OBS), -1.0, F32)
    sends = [jnp.concatenate(parts + [spare], axis=1) for parts in sends]
    slot = iota((SLOTS, BLK), 0).astype(F32)
    for part in range(0, PARTS, 2):
        tiles = []
        for at in (part, part + 1):
            for side in range(3):
                tiles.append(jnp.where(sends[side] == slot + float(at * SENT + side * SLOTS), 1.0, 0.0))
        choice_ref[pl.ds(part * SENT, 2 * SENT), :] = jnp.concatenate(tiles, axis=0).astype(BF16)


def spread(tmp_ref, field):
    for run in range(LON // BLK):
        tmp_ref[run] = field[:, run * BLK : (run + 1) * BLK]
    tail = LON % BLK
    tmp_ref[LON // BLK] = jnp.concatenate(
        [field[:, LON - tail :], field[:, :PAD], field[:, LON - PAD :]], axis=1
    )


def spread_row(tmp_ref, row):
    return jnp.concatenate(
        [tmp_ref[run, pl.ds(row, LEV, stride=ROWS), :] for run in range(WIDE // BLK)], axis=1
    )


def put_row(tmp_ref, row, value):
    for run in range(WIDE // BLK):
        tmp_ref[run, pl.ds(row, LEV, stride=ROWS), :] = value[:, run * BLK : (run + 1) * BLK]


def gathered(tmp_ref):
    return jnp.concatenate([tmp_ref[run] for run in range(WIDE // BLK)], axis=1)[:, :LON]


def edges_body(inc_hbm, wts_hbm, err_hbm, val_hbm, wt_hbm, out_ref, own_ref, aux_ref, err_ref, sems):
    for copy in copies(
        sems,
        (inc_hbm, own_ref.at[pl.ds(0, FIELD)]),
        (wts_hbm, own_ref.at[pl.ds(FIELD, 4 * ROWS)]),
        (err_hbm, err_ref),
        (val_hbm, aux_ref.at[pl.ds(0, ALL_OBS)]),
        (wt_hbm, aux_ref.at[pl.ds(ALL_OBS, ALL_OBS)]),
    ):
        copy.wait()
    out_ref[0 : FIELD + 4 * ROWS, :] = own_ref[...].astype(BF16)
    out_ref[FIELD + 4 * ROWS : SENT_ROWS, :] = err_ref[...].astype(BF16)


def widen(value):
    tail = LON % BLK
    return jnp.concatenate(
        [value[:, : LON - tail], jnp.concatenate([value[:, LON - tail :], value[:, :PAD], value[:, LON - PAD :]], axis=1)],
        axis=1,
    )


def row_of(ref, which, row):
    return jnp.broadcast_to(ref[which, pl.ds(row, 1), :], (LEV, WIDE))


def forward_body(
    own_hbm, south_ref, north_ref, t1_ref, t2_ref, t3_ref, t4_ref, last_ref, next_ref, pack_ref,
    x_ref, flat_ref, wide_ref, low_tmp, own_tmp, high_tmp, own_ref, sems,
):
    (wait,) = copies(sems, (own_hbm, own_ref))
    spread(low_tmp, south_ref[FIELD + 4 * ROWS :, :].astype(F32))
    spread(high_tmp, north_ref[FIELD + 4 * ROWS :, :].astype(F32))
    for row in range(HALO):
        pack_ref[EXT + row] = spread_row(low_tmp, HALO + row)
        pack_ref[EXT + HALO + row] = spread_row(high_tmp, row)
    spread(low_tmp, south_ref[0:FIELD, :].astype(F32))
    spread(high_tmp, north_ref[0:FIELD, :].astype(F32))
    for row in range(ROWS):
        x_ref[row] = spread_row(low_tmp, row)
        x_ref[2 * ROWS + row] = spread_row(high_tmp, row)
    wait.wait()
    spread(own_tmp, own_ref[0:FIELD, :])
    for row in range(ROWS):
        x_ref[ROWS + row] = spread_row(own_tmp, row)
    for side in range(4):
        rows = slice(FIELD + side * ROWS, FIELD + (side + 1) * ROWS)
        for i, part_ref in enumerate((south_ref, own_ref, north_ref)):
            wide_ref[side + 1, i * ROWS : (i + 1) * ROWS, :] = widen(part_ref[rows, :].astype(F32))
    wide_ref[0] = 1.0 - (wide_ref[1] + wide_ref[2] + wide_ref[3] + wide_ref[4])
    for side in range(5):
        for half in range(2):
            first = HALO + half * ROWS
            pack_ref[EXT + ROWS + 2 * side + half] = wide_ref[side, first : first + ROWS, :]
    for row in range(0, EXT, 2):
        pair = [x_ref[HALO + row + i][:, :LON] for i in range(2)]
        next_ref[pl.ds(row * LEV, 2 * LEV), :] = jnp.concatenate(pair, axis=0).astype(BF16)

    for step in range(STEPS):
        old, new = (step % 2) * FULL, ((step + 1) % 2) * FULL
        for row in range(step + 1, FULL - step - 1):
            v = x_ref[old + row]
            moved = (
                row_of(wide_ref, 0, row) * v
                + row_of(wide_ref, 1, row) * pltpu.roll(v, WIDE - 1, 1)
                + row_of(wide_ref, 2, row) * pltpu.roll(v, 1, 1)
                + row_of(wide_ref, 3, row) * x_ref[old + row + 1]
                + row_of(wide_ref, 4, row) * x_ref[old + row - 1]
            )
            own = row - ROWS
            if step < STEPS - 1:
                x_ref[new + row] = moved
            else:
                pack_ref[row - HALO] = moved
                if 0 <= own < ROWS:
                    put_row(own_tmp, own, moved)
            if 0 <= own < ROWS:
                part = own % 4
                flat_ref[own // 4, :, part * LON : (part + 1) * LON] = moved[:, :LON]
        for pair in range(HALF):
            tiles = []
            for tile in (2 * pair, 2 * pair + 1):
                half, at = tile // HALF, tile % HALF
                tiles.append(flat_ref[half, :, at * BLK : (at + 1) * BLK])
            (t1_ref, t2_ref, t3_ref, t4_ref)[step][pl.ds(pair * 2 * LEV, 2 * LEV), :] = jnp.concatenate(tiles, axis=0).astype(BF16)
    last_ref[...] = gathered(own_tmp).astype(BF16)


def gather_body(asked_ref, t1_ref, t2_ref, t3_ref, t4_ref, out_ref, token_ref, slots_ref):
    lane = iota((PARTS, BLOCKS), 1)
    asked = asked_ref[...]
    for step in range(STEPS):
        picks = [
            jnp.where(asked[:, 2 * step + nth : 2 * step + nth + 1] == lane, 1.0, 0.0).astype(BF16)
            for nth in range(2)
        ]
        blocks = jnp.dot(jnp.concatenate(picks, axis=0), (t1_ref, t2_ref, t3_ref, t4_ref)[step][...], preferred_element_type=F32)
        for nth in range(2):
            slots_ref[pl.ds(2 * step + nth, PARTS, stride=SLOTS), :] = blocks[nth * PARTS : (nth + 1) * PARTS]
    out_ref[...] = slots_ref[...].astype(BF16)
    token_ref[...] = slots_ref[0:8, :]


def hold_body(token_ref, last_in, next_in, last_out, next_out, seen_ref):
    seen_ref[...] = token_ref[...]


def spread_out(block):
    line = iota(block.shape, 0)
    zero = jnp.zeros_like(block)
    return jnp.concatenate([jnp.where(line == i, block, zero) for i in range(block.shape[0])], axis=1)


GROUP = 16


def observe_body(
    got_ref, choice_hbm, aux_hbm, ops_hbm, _, dep_ref, out_ref, choice_ref, aux_ref, ops_ref, sems
):
    size = GROUP * BLK
    parts = [pl.ds(first, size) for first in range(0, ALL_OBS * BLK, size)]
    pairs = [(choice_hbm, choice_ref), (aux_hbm, aux_ref)]
    waits = copies(sems, *pairs, *[(ops_hbm.at[part], ops_ref.at[part]) for part in parts])
    waits[0].wait()
    base = PARTS * SENT
    pick = jnp.concatenate([choice_ref[base + half * ALL_OBS : base + (half + 1) * ALL_OBS, :] for half in range(2)], axis=1)
    seen = jnp.dot(pick, got_ref[...], preferred_element_type=F32).astype(BF16)
    waits[1].wait()
    line = iota((GROUP, BLK), 0)
    scaled = []
    for at in range(ALL_OBS // GROUP):
        waits[2 + at].wait()
        first = at * GROUP
        rows = slice(first, first + GROUP)
        product = jnp.zeros((GROUP, BLK), F32)
        for i in range(0, GROUP, 2):
            two = lax.dot_general(
                seen[rows],
                ops_ref[(first + i) * BLK : (first + i + 2) * BLK, :],
                (((1,), (1,)), ((), ())),
                preferred_element_type=F32,
            )
            product = jnp.where(line == i, two[:, :BLK], product)
            product = jnp.where(line == i + 1, two[:, BLK:], product)
        departure = product - aux_ref[first : first + GROUP, :]
        dep_ref[rows, :] = departure
        weight = aux_ref[ALL_OBS + first : ALL_OBS + first + GROUP, :]
        scaled.append((weight * departure).astype(BF16))
    steps = []
    for at, block in enumerate(scaled):
        first = at * GROUP
        steps.append(
            jnp.dot(
                spread_out(block), ops_ref[first * BLK : (first + GROUP) * BLK, :], preferred_element_type=F32
            ).astype(BF16)
        )
    increments = jnp.concatenate(steps, axis=0)
    out_ref[...] = jnp.dot(choice_ref[:base, :ALL_OBS], increments, preferred_element_type=F32).astype(BF16)


PAIRS = ((2, 3), (0, 1))
SIDES = ((0, 0, 0, BLOCKS), (1, BLOCKS, HALF * LEV, HALF * LEV), (2, BLOCKS + HALF * LEV, 0, HALF * LEV))


def put_body(asked_ref, late_ref, early_ref):
    asked = jnp.transpose(asked_ref[...].astype(F32))
    for at, steps in enumerate(PAIRS):
        for side, base, start, size in SIDES:
            named = jnp.concatenate(
                [asked[side * SLOTS + 2 * step + nth :][:1] for step in steps for nth in range(2)], axis=1
            )
            line = (iota((size, 4 * PARTS), 0) + start).astype(F32)
            (late_ref, early_ref)[at][base : base + size, :] = jnp.where(line == named, 1.0, 0.0).astype(BF16)


def prepare_body(
    next_ref, err_ref, dep_ref, pack_hbm, a_ref, b_ref, c_ref, d_ref, out_ref, *rest
):
    *coef_refs, own_tmp, pack_ref, sems = rest
    (wait,) = copies(sems, (pack_hbm, pack_ref))
    out_ref[...] = dep_ref[...]
    spread(own_tmp, err_ref[...])
    wait.wait()
    final = lax.axis_index("tm") == lax.axis_size("tm") - 1
    for row in range(0, EXT, 2):
        both = next_ref[pl.ds(row * LEV, 2 * LEV), :].astype(F32)
        for i in range(2):
            at = row + i - HALO
            if 0 <= at < ROWS:
                weight = spread_row(own_tmp, at)
            else:
                weight = pack_ref[EXT + (row + i) % ROWS]
            ahead = weight * (pack_ref[row + i] - widen(both[i * LEV : (i + 1) * LEV]))
            (a_ref, b_ref, c_ref, d_ref)[row // 4][(row + i) % 4] = jnp.where(final, 0.0, ahead)
    for which, coef_ref in enumerate(coef_refs):
        for half in range(2):
            coef_ref[half * ROWS : (half + 1) * ROWS, :] = pack_ref[EXT + ROWS + 2 * which + half]


def adjoint_body(got_ref, prev_ref, late_ref, early_ref, *rest):
    first_refs, coef_refs = rest[:4], rest[4:9]
    inc_hbm, err_hbm, back_hbm, out_ref, got_f, flat_ref, a_ref, y_ref, tmp_ref, inc_ref, err_ref, back_ref, sems = rest[9:]
    waits = copies(sems, (inc_hbm, inc_ref), (err_hbm, err_ref), (back_hbm, back_ref))

    def weight(which, row):
        return jnp.broadcast_to(coef_refs[which][pl.ds(row, 1), :], (LEV, WIDE))

    got_f[...] = got_ref[...].astype(F32)
    for at, steps in enumerate(PAIRS):
        for side, base, start, size in SIDES:
            sides = []
            for i, step in enumerate(steps):
                terms = jnp.concatenate(
                    [got_f[pl.ds(side * SLOTS + 2 * step + nth, PARTS, stride=SENT), :] for nth in range(2)], axis=0
                ).astype(BF16)
                zero = jnp.zeros_like(terms)
                sides.append(jnp.concatenate([terms, zero] if i == 0 else [zero, terms], axis=0))
            added = jnp.dot(
                (late_ref, early_ref)[at][base : base + size, :],
                jnp.concatenate(sides, axis=1),
                preferred_element_type=F32
            )
            flat = (1, 0, 3)[side]
            for i, step in enumerate(steps):
                for tile in range(size // LEV):
                    half, run = tile // HALF, tile % HALF
                    flat_ref[step * 4 + flat + half, :, run * BLK : (run + 1) * BLK] = added[
                        tile * LEV : (tile + 1) * LEV, i * BLK : (i + 1) * BLK
                    ]
    for step in range(STEPS - 1, -1, -1):
        edge = STEPS - 1 - step
        for row in range(edge, EXT - edge):
            part = row % 4
            before = first_refs[row // 4][row % 4] if edge == 0 else y_ref[row]
            a_ref[row] = before + widen(flat_ref[step * 4 + row // 4, :, part * LON : (part + 1) * LON])
        for row in range(edge + 1, EXT - edge - 1):
            v = a_ref[row]
            pulled = (
                weight(0, row) * v
                + pltpu.roll(weight(1, row) * v, 1, 1)
                + pltpu.roll(weight(2, row) * v, WIDE - 1, 1)
                + weight(3, row - 1) * a_ref[row - 1]
                + weight(4, row + 1) * a_ref[row + 1]
            )
            if step:
                y_ref[row] = pulled
            else:
                put_row(tmp_ref, row - HALO, pulled)
    for wait in waits:
        wait.wait()
    begin = jnp.where(lax.axis_index("tm") == 0, back_ref[...], prev_ref[...].astype(F32))
    out_ref[...] = gathered(tmp_ref) + err_ref[...] * (inc_ref[...] - begin)


def shape(dims, dtype):
    return jax.ShapeDtypeStruct(dims, dtype)


def exchange(block):
    return lax.all_to_all(block, "space", split_axis=0, concat_axis=0, tiled=True)


def local(
    increments,
    background,
    error_weight,
    neighbor_weights,
    operators,
    values,
    obs_weight,
    owners,
    columns,
):
    fields = LEV * ROWS
    start = increments.reshape(fields, LON)
    owner = owners.reshape(STEPS, 1, OBS)
    windows, parts = lax.axis_size("tm"), lax.axis_size("space")
    vmem = pl.BlockSpec(memory_space=pltpu.VMEM)
    home = pl.BlockSpec(memory_space=pltpu.HBM)
    anywhere = pl.BlockSpec(memory_space=pl.ANY)
    sems = pltpu.SemaphoreType.DMA
    field = pltpu.VMEM((fields, LON), F32)
    runs = pltpu.VMEM((WIDE // BLK, fields, BLK), F32)
    wide = pltpu.VMEM((EXT, LEV, WIDE), F32)

    err = error_weight.reshape(fields, LON)
    stencil = neighbor_weights.reshape(4 * ROWS, LON)
    edge, own, aux = pl.pallas_call(
        edges_body,
        in_specs=[home] * 5,
        out_shape=(
            shape((SENT_ROWS, LON), BF16),
            shape((FIELD + 4 * ROWS, LON), F32),
            shape((2 * ALL_OBS, BLK), F32),
        ),
        scratch_shapes=[field, sems((5,))],
        name="edges",
        compiler_params=params(60),
    )(start, stencil, err, values.reshape(ALL_OBS, BLK), obs_weight.reshape(ALL_OBS, BLK))
    south = lax.ppermute(edge, "space", [(i, i + 1) for i in range(parts - 1)])
    north = lax.ppermute(edge, "space", [(i + 1, i) for i in range(parts - 1)])

    request, choice = pl.pallas_call(
        request_body,
        in_specs=[home, home, anywhere],
        out_shape=(
            shape((PARTS, BLK), I32),
            shape((PARTS * SENT + 2 * ALL_OBS, BLK), BF16),
        ),
        scratch_shapes=[pltpu.VMEM((STEPS, 1, OBS), I32), pltpu.VMEM((STEPS, OBS), I32), sems((2,))],
        name="request",
        compiler_params=params(60),
    )(owner, columns.reshape(STEPS, OBS), aux)
    asked = exchange(request)

    around = shape((EXT * LEV, LON), BF16)
    here = shape((fields, LON), BF16)
    *tables, last, following, pack = pl.pallas_call(
        forward_body,
        in_specs=[home, vmem, vmem],
        out_shape=(
            *[shape((BLOCKS, BLK), BF16) for _ in range(STEPS)],
            here,
            around,
            shape((EXT + ROWS + 10, LEV, WIDE), F32),
        ),
        scratch_shapes=[
            pltpu.VMEM((2 * FULL, LEV, WIDE), F32),
            pltpu.VMEM((2, LEV, HALF * BLK), F32),
            pltpu.VMEM((5, FULL, WIDE), F32),
            runs,
            runs,
            runs,
            pltpu.VMEM((FIELD + 4 * ROWS, LON), F32),
            sems((1,)),
        ],
        name="forward",
        compiler_params=params(51.45),
    )(own, south, north)

    mark = shape((8, BLK), F32)
    blocks, token = pl.pallas_call(
        gather_body,
        out_shape=(shape((PARTS * SLOTS, BLK), BF16), mark),
        scratch_shapes=[pltpu.VMEM((PARTS * SLOTS, BLK), F32)],
        name="gather",
        compiler_params=params(16),
    )(asked, *tables)
    got = exchange(blocks)

    last, following, token = pl.pallas_call(
        hold_body,
        in_specs=[vmem, anywhere, anywhere],
        out_specs=(anywhere, anywhere, vmem),
        out_shape=(here, around, mark),
        input_output_aliases={1: 0, 2: 1},
        name="hold",
        cost_estimate=pl.CostEstimate(flops=0, transcendentals=0, bytes_accessed=30_000_000),
        compiler_params=params(16),
    )(token, last, following)
    previous = lax.ppermute(last, "tm", [(i, i + 1) for i in range(windows - 1)])
    following = lax.ppermute(following, "tm", [(i + 1, i) for i in range(windows - 1)])

    per_obs = shape((ALL_OBS, BLK), F32)
    found, slots = pl.pallas_call(
        observe_body,
        in_specs=[vmem] + [home] * 3 + [anywhere],
        out_shape=(per_obs, shape((PARTS * SENT, BLK), BF16)),
        scratch_shapes=[
            pltpu.VMEM((PARTS * SENT + 2 * ALL_OBS, BLK), BF16),
            pltpu.VMEM((2 * ALL_OBS, BLK), F32),
            pltpu.VMEM((ALL_OBS * BLK, BLK), BF16),
            sems((2 + ALL_OBS // GROUP,)),
        ],
        name="observe",
        compiler_params=params(53.75),
    )(got, choice, aux, operators.reshape(ALL_OBS * BLK, BLK), following)
    arrived = exchange(slots)

    half = shape((2 * BLOCKS, BLK), BF16)
    put = pl.pallas_call(put_body, out_shape=(half, half), name="put", compiler_params=params(16))(asked)
    quarter = shape((4, LEV, WIDE), F32)
    *ahead, departures, c, e, w, n, q = pl.pallas_call(
        prepare_body,
        in_specs=[vmem] * 3 + [home],
        out_shape=(*[quarter] * 4, per_obs, *[shape((EXT, WIDE), F32)] * 5),
        scratch_shapes=[runs, pltpu.VMEM((EXT + ROWS + 10, LEV, WIDE), F32), sems((1,))],
        name="prepare",
        compiler_params=params(51.5),
    )(following, err, found, pack)

    gradient = pl.pallas_call(
        adjoint_body,
        in_specs=[vmem] * 13 + [home] * 3,
        out_shape=shape((fields, LON), F32),
        scratch_shapes=[
            pltpu.VMEM((PARTS * SENT, BLK), F32),
            pltpu.VMEM((4 * STEPS, LEV, HALF * BLK), F32),
            wide,
            wide,
            runs,
            field,
            field,
            field,
            sems((3,)),
        ],
        name="adjoint",
        compiler_params=params(51.45),
    )(arrived, previous, *put, *ahead, c, e, w, n, q, start, err, background.reshape(fields, LON))
    return (gradient.reshape(increments.shape), departures.reshape(values.shape))


def solution(mesh):
    in_specs = (
        P("tm", None, "space", None),
        P(None, "space", None),
        P(None, "space", None),
        P(None, "space", None),
        P("tm", None, "space", None, None),
        P("tm", None, "space", None),
        P("tm", None, "space", None),
        P("tm", None, "space", None),
        P("tm", None, "space"),
    )
    out_specs = (P("tm", None, "space", None), P("tm", None, "space", None))
    return jax.shard_map(local, mesh=mesh, in_specs=in_specs, out_specs=out_specs, check_vma=False)
```

time: 81 us -> 77.3 us (0.954)
  the two profiles are of different devices: /device:TPU:223 before, /device:TPU:320 now
where the time goes in v2:
time: 77.3 us; the launch traced here: 76.8 us
  starting transfers between devices  24.4 us (32%)
  Pallas kernels  22 us (28%)
  blocking collectives  18.7 us (24%)
  waiting for transfers between devices  9.23 us (12%)
  local copies, waits for them, and re-layouts  1.74 us (2%)
    all_to_all x1, blocking collectives, exchange(): lax.all_to_all(block, 'space', split_axis=0, concat_axis=0, tiled=True)  18.7 us
    all_to_all x2, starting transfers between devices, exchange(): lax.all_to_all(block, 'space', split_axis=0, concat_axis=0, tiled=True)  15.8 us
    all_to_all x2, waiting for transfers between devices, exchange(): lax.all_to_all(block, 'space', split_axis=0, concat_axis=0, tiled=True)  7.58 us
    pallas_call x1, Pallas kernels, local(): pl.pallas_call(forward_body, in_specs=[home, vmem, vmem], out_shape=(*[sh...  6.5 us
    pallas_call x1, Pallas kernels, local(): pl.pallas_call(observe_body, in_specs=[vmem] + [home] * 3 + [anywhere], o...  4.1 us
    pallas_call x1, Pallas kernels, local(): pl.pallas_call(adjoint_body, in_specs=[vmem] * 13 + [home] * 3, out_shape...  4.06 us
    ppermute x1, starting transfers between devices, local(): south = lax.ppermute(edge, 'space', [(i, i + 1) for i in range(parts - 1)])  3.43 us
    pallas_call x1, Pallas kernels, local(): pl.pallas_call(edges_body, in_specs=[home] * 5, out_shape=(shape((SENT_RO...  2.28 us
  transfers between devices with their start and end apart: 6, of which 3 were waited for; matrix products, arithmetic and copies ran while one was open for 0% of the time, Pallas kernels for 14%

profile of v2, /device:TPU:320, one launch (start us, length us, event | category | flops | bytes accessed | tf_op | source)
XLA Modules:
  0.0 76.8 jit_solution(17744915999371776290)
XLA Ops:
  0.6 2.3 %edges.1 = (bf16[160,1440]{1,0:T(8,128)(2,1)}, f32[96,1440]{1,0:T(8,128)}, f32[192,128]{1,0:T(8,128)}) custom-call(f32[64,1440]{1,0:T(8,128)} %bitcast.30, f32[32,1440]{1,0:T(8,128)} %bitcast.35, f32[64,1440]{1,0:T(8,128)} %bitcast.21, f32[96,128]{1,0:T(8,128)} %bitcast.36, f32[96,128]{1,0:T(8,128)} %bitcast.37), custom_call_target="tpu_custom_call" | custom-call | tf_op jit(solution)/shard_map/edges/pallas_call | solution.py:409
  2.9 3.4 %collective-permute-start = (bf16[160,1440]{1,0:T(8,128)(2,1)}, bf16[160,1440]{1,0:T(8,128)(2,1)S(1)}, u32[]{:S(2)}, u32[]{:S(2)}) collective-permute-start(bf16[160,1440]{1,0:T(8,128)(2,1)} %get-tuple-element.35), channel_id=1, source_target_pairs={{0,1},{1,2},{2,3},{3,4},{4,5},{5,6},{6,7},{7,8},{8,9},{9,10},{10,1... | collective-permute-start | bytes 1382408 | tf_op jit(solution)/shard_map/ppermute | solution.py:421
  6.4 1.3 %collective-permute-start.1 = (bf16[160,1440]{1,0:T(8,128)(2,1)}, bf16[160,1440]{1,0:T(8,128)(2,1)S(1)}, u32[]{:S(2)}, u32[]{:S(2)}) collective-permute-start(bf16[160,1440]{1,0:T(8,128)(2,1)} %get-tuple-element.35), channel_id=1, source_target_pairs={{1,0},{2,1},{3,2},{4,3},{5,4},{6,5},{7,6},{8,7},{9,8},{10,9},{11,1... | collective-permute-start | bytes 1382408 | tf_op jit(solution)/shard_map/ppermute | solution.py:422
  7.7 1.7 %request.1 = (s32[32,128]{1,0:T(8,128)}, bf16[960,128]{1,0:T(8,128)(2,1)}) custom-call(s32[4,1,24]{2,1,0:T(1,128)} %bitcast.39, s32[4,24]{1,0:T(4,128)} %bitcast.40, f32[192,128]{1,0:T(8,128)} %get-tuple-element.32._.aux_hbm), custom_call_target="tpu_custom_call" | custom-call | tf_op jit(solution)/shard_map/request/pallas_call | solution.py:424
  9.4 11.9 %all-to-all-start = ((s32[32,1,128]{2,1,0:T(1,128)}), s32[32,1,128]{2,1,0:T(1,128)S(1)}, u32[]{:S(2)}, u32[]{:S(2)}) async-start(s32[32,1,128]{2,1,0:T(1,128)} %bitcast.38), calls=%async_computation | async-start | bytes 32768 | tf_op jit(solution)/shard_map/all_to_all | solution.py:381
  21.3 0.0 collective-permute-done.south_ref
  21.3 0.0 collective-permute-done.1.north_ref
  21.4 6.5 %forward.1 = (bf16[720,128]{1,0:T(8,128)(2,1)S(1)}, bf16[720,128]{1,0:T(8,128)(2,1)S(1)}, bf16[720,128]{1,0:T(8,128)(2,1)S(1)}, bf16[720,128]{1,0:T(8,128)(2,1)S...) custom-call(f32[96,1440]{1,0:T(8,128)} %get-tuple-element.34.own_hbm, ...), custom_call_target="tpu_custom_call" | custom-call | tf_op jit(solution)/shard_map/forward/pallas_call | solution.py:439
  27.9 0.0 copy-start
  27.9 3.1 %all-to-all-done = s32[32,1,128]{2,1,0:T(1,128)S(1)} async-done(((s32[32,1,128]{2,1,0:T(1,128)}), s32[32,1,128]{2,1,0:T(1,128)S(1)}, u32[]{:S(2)}, u32[]{:S(2)}) %all-to-all-start) | async-done | bytes 16416 | tf_op jit(solution)/shard_map/all_to_all | solution.py:381
  31.0 0.3 gather.1
  31.3 0.6 hold.1
  31.9 1.9 %collective-permute-start.2 = (bf16[128,1440]{1,0:T(8,128)(2,1)S(1)}, bf16[128,1440]{1,0:T(8,128)(2,1)S(1)}, u32[]{:S(2)}, u32[]{:S(2)}) collective-permute-start(bf16[128,1440]{1,0:T(8,128)(2,1)S(1)} %get-tuple-element.45), channel_id=1, source_target_pairs={{32,0},{64,32},{96,64},{128,96},{160,128},{192,160},{224,192},{256... | collective-permute-start | bytes 1105928 | tf_op jit(solution)/shard_map/ppermute | solution.py:483
  33.8 18.7 %all_to_all.33 = bf16[32,8,128]{2,1,0:T(8,128)(2,1)S(1)} all-to-all(bf16[32,8,128]{2,1,0:T(8,128)(2,1)S(1)} %bitcast.28), channel_id=1, replica_groups=mesh['tm'=16,'space'=32] {'space'}, dimensions={0} | all-to-all | bytes 131072 | tf_op jit(solution)/shard_map/all_to_all | solution.py:381
  52.6 0.0 collective-permute-done.2._.next_ref
  52.6 0.0 copy-start.1
  52.6 0.7 copy-done.1
  53.3 4.1 %observe.1 = (f32[96,128]{1,0:T(8,128)S(1)}, bf16[768,128]{1,0:T(8,128)(2,1)}) custom-call(bf16[256,128]{1,0:T(8,128)(2,1)S(1)} %bitcast.25, bf16[960,128]{1,0:T(8,128)(2,1)} %get-tuple-element.41.choice_hbm, f32[192,128]{1,0:T(8,128)} %get-tuple-element.32._.aux_hbm, bf16[12288,128]{1,0:T(8,128)(2,1)} %bitcast.29, bf16[128,1440]{1,0:T(8,128)(2,1)} %copy-done.1), custom_call_target="tpu_custom_call" | custom-call | tf_op jit(solution)/shard_map/observe/pallas_call | solution.py:486
  57.4 3.9 %all-to-all-start.2 = ((bf16[32,24,128]{2,1,0:T(8,128)(2,1)}), bf16[32,24,128]{2,1,0:T(8,128)(2,1)S(1)}, u32[]{:S(2)}, u32[]{:S(2)}) async-start(bf16[32,24,128]{2,1,0:T(8,128)(2,1)} %bitcast.34), calls=%async_computation.2 | async-start | bytes 393216 | tf_op jit(solution)/shard_map/all_to_all | solution.py:381
  61.3 1.9 %collective-permute-start.3 = (bf16[64,1440]{1,0:T(8,128)(2,1)S(1)}, bf16[64,1440]{1,0:T(8,128)(2,1)S(1)}, u32[]{:S(2)}, u32[]{:S(2)}) collective-permute-start(bf16[64,1440]{1,0:T(8,128)(2,1)S(1)} %get-tuple-element.47), channel_id=1, source_target_pairs={{0,32},{32,64},{64,96},{96,128},{128,160},{160,192},{192,224},{224... | collective-permute-start | bytes 552968 | tf_op jit(solution)/shard_map/ppermute | solution.py:482
  63.2 0.3 put.1
  63.5 0.0 copy-done
  63.5 0.0 copy-start.2
  63.6 1.0 %copy-done.2 = bf16[128,1440]{1,0:T(8,128)(2,1)S(1)} copy-done((bf16[128,1440]{1,0:T(8,128)(2,1)S(1)}, bf16[128,1440]{1,0:T(8,128)(2,1)}, u32[]{:S(2)}) %copy-start.2) | copy-done | bytes 368664
  64.5 2.1 %prepare.1 = (f32[4,8,1536]{2,1,0:T(8,128)S(1)}, f32[4,8,1536]{2,1,0:T(8,128)S(1)}, f32[4,8,1536]{2,1,0:T(8,128)S(1)}, f32[4,8,1536]{2,1,0:T(8,128)S(1)}, f32[96...) custom-call(bf16[128,1440]{1,0:T(8,128)(2,1)S(1)} %copy-done.2, ...), custom_call_target="tpu_custom_call" | custom-call | tf_op jit(solution)/shard_map/prepare/pallas_call | solution.py:504
  66.6 1.6 %collective-permute-done.3.prev_ref = bf16[64,1440]{1,0:T(8,128)(2,1)S(1)} collective-permute-done((bf16[64,1440]{1,0:T(8,128)(2,1)S(1)}, bf16[64,1440]{1,0:T(8,128)(2,1)S(1)}, u32[]{:S(2)}, u32[]{:S(2)}) %collective-permute-start.3) | collective-permute-done | bytes 184352 | tf_op jit(solution)/shard_map/ppermute | solution.py:482
  68.3 4.5 %all-to-all-done.2 = bf16[32,24,128]{2,1,0:T(8,128)(2,1)S(1)} async-done(((bf16[32,24,128]{2,1,0:T(8,128)(2,1)}), bf16[32,24,128]{2,1,0:T(8,128)(2,1)S(1)}, u32[]{:S(2)}, u32[]{:S(2)}) %all-to-all-start.2) | async-done | bytes 196640 | tf_op jit(solution)/shard_map/all_to_all | solution.py:381
  72.7 4.1 %adjoint.1 = f32[64,1440]{1,0:T(8,128)} custom-call(bf16[768,128]{1,0:T(8,128)(2,1)S(1)} %bitcast.24, bf16[64,1440]{1,0:T(8,128)(2,1)S(1)} %collective-permute-done.3.prev_ref, bf16[1440,128]{1,0:T(8,128)(2,1)S(1)} %get-tuple-element.48.late_ref, bf16[1440,128]{1,0:T(8,128)(2,1)S(1)} %get-tuple-element.49.early_ref, ...), custom_call_target="tpu_custom_call" | custom-call | tf_op jit(solution)/shard_map/adjoint/pallas_call | solution.py:513
Async XLA Ops:
  2.9 18.4 %collective-permute-start = (bf16[160,1440]{1,0:T(8,128)(2,1)}, bf16[160,1440]{1,0:T(8,128)(2,1)S(1)}, u32[]{:S(2)}, u32[]{:S(2)}) collective-permute-start(bf16[160,1440]{1,0:T(8,128)(2,1)} %get-tuple-element.35), channel_id=1, source_target_pairs={{0,1},{1,2},{2,3},{3,4},{4,5},{5,6},{6,7},{7,8},{8,9},{9,10},{10,1... | collective-permute-start | bytes 1382408 | tf_op jit(solution)/shard_map/ppermute | solution.py:421
  6.4 15.0 %collective-permute-start.1 = (bf16[160,1440]{1,0:T(8,128)(2,1)}, bf16[160,1440]{1,0:T(8,128)(2,1)S(1)}, u32[]{:S(2)}, u32[]{:S(2)}) collective-permute-start(bf16[160,1440]{1,0:T(8,128)(2,1)} %get-tuple-element.35), channel_id=1, source_target_pairs={{1,0},{2,1},{3,2},{4,3},{5,4},{6,5},{7,6},{8,7},{9,8},{10,9},{11,1... | collective-permute-start | bytes 1382408 | tf_op jit(solution)/shard_map/ppermute | solution.py:422
  9.4 21.6 %all-to-all-start = ((s32[32,1,128]{2,1,0:T(1,128)}), s32[32,1,128]{2,1,0:T(1,128)S(1)}, u32[]{:S(2)}, u32[]{:S(2)}) async-start(s32[32,1,128]{2,1,0:T(1,128)} %bitcast.38), calls=%async_computation | async-start | bytes 32768 | tf_op jit(solution)/shard_map/all_to_all | solution.py:381
  27.9 35.7 %copy-start = (f32[8,8,1440]{2,1,0:T(8,128)S(1)}, f32[8,8,1440]{2,1,0:T(8,128)}, u32[]{:S(2)}) copy-start(f32[8,8,1440]{2,1,0:T(8,128)} %param.11) | copy-start | bytes 1105924
  31.9 20.6 %collective-permute-start.2 = (bf16[128,1440]{1,0:T(8,128)(2,1)S(1)}, bf16[128,1440]{1,0:T(8,128)(2,1)S(1)}, u32[]{:S(2)}, u32[]{:S(2)}) collective-permute-start(bf16[128,1440]{1,0:T(8,128)(2,1)S(1)} %get-tuple-element.45), channel_id=1, source_target_pairs={{32,0},{64,32},{96,64},{128,96},{160,128},{192,160},{224,192},{256... | collective-permute-start | bytes 1105928 | tf_op jit(solution)/shard_map/ppermute | solution.py:483
  52.6 0.7 copy-start.1
  57.4 15.3 %all-to-all-start.2 = ((bf16[32,24,128]{2,1,0:T(8,128)(2,1)}), bf16[32,24,128]{2,1,0:T(8,128)(2,1)S(1)}, u32[]{:S(2)}, u32[]{:S(2)}) async-start(bf16[32,24,128]{2,1,0:T(8,128)(2,1)} %bitcast.34), calls=%async_computation.2 | async-start | bytes 393216 | tf_op jit(solution)/shard_map/all_to_all | solution.py:381
  61.3 7.0 %collective-permute-start.3 = (bf16[64,1440]{1,0:T(8,128)(2,1)S(1)}, bf16[64,1440]{1,0:T(8,128)(2,1)S(1)}, u32[]{:S(2)}, u32[]{:S(2)}) collective-permute-start(bf16[64,1440]{1,0:T(8,128)(2,1)S(1)} %get-tuple-element.47), channel_id=1, source_target_pairs={{0,32},{32,64},{64,96},{96,128},{128,160},{160,192},{192,224},{224... | collective-permute-start | bytes 552968 | tf_op jit(solution)/shard_map/ppermute | solution.py:482
  63.5 1.0 %copy-start.2 = (bf16[128,1440]{1,0:T(8,128)(2,1)S(1)}, bf16[128,1440]{1,0:T(8,128)(2,1)}, u32[]{:S(2)}) copy-start(bf16[128,1440]{1,0:T(8,128)(2,1)} %copy-done.1) | copy-start | bytes 1105924

commit v3 on v2

--- a/solution.py
+++ b/solution.py
@@ -15,7 +15,7 @@
 EXT = ROWS + 2 * HALO
 FULL = 3 * ROWS
 FIELD = LEV * ROWS
-SENT_ROWS = FIELD + 4 * ROWS + FIELD
+SENT_ROWS = FIELD + 4 * ROWS + LEV * HALO
 OBS = 24
 ALL_OBS = STEPS * OBS
 BLK = 128
@@ -97,16 +97,16 @@
 
 def spread(tmp_ref, field):
     for run in range(LON // BLK):
-        tmp_ref[run] = field[:, run * BLK : (run + 1) * BLK]
+        tmp_ref[run, : field.shape[0], :] = field[:, run * BLK : (run + 1) * BLK]
     tail = LON % BLK
-    tmp_ref[LON // BLK] = jnp.concatenate(
+    tmp_ref[LON // BLK, : field.shape[0], :] = jnp.concatenate(
         [field[:, LON - tail :], field[:, :PAD], field[:, LON - PAD :]], axis=1
     )
 
 
-def spread_row(tmp_ref, row):
+def spread_row(tmp_ref, row, apart=ROWS):
     return jnp.concatenate(
-        [tmp_ref[run, pl.ds(row, LEV, stride=ROWS), :] for run in range(WIDE // BLK)], axis=1
+        [tmp_ref[run, pl.ds(row, LEV, stride=apart), :] for run in range(WIDE // BLK)], axis=1
     )
 
 
@@ -119,7 +119,7 @@
     return jnp.concatenate([tmp_ref[run] for run in range(WIDE // BLK)], axis=1)[:, :LON]
 
 
-def edges_body(inc_hbm, wts_hbm, err_hbm, val_hbm, wt_hbm, out_ref, own_ref, aux_ref, err_ref, sems):
+def edges_body(inc_hbm, wts_hbm, err_hbm, val_hbm, wt_hbm, low_ref, high_ref, own_ref, aux_ref, err_ref, sems):
     for copy in copies(
         sems,
         (inc_hbm, own_ref.at[pl.ds(0, FIELD)]),
@@ -129,8 +129,13 @@
         (wt_hbm, aux_ref.at[pl.ds(ALL_OBS, ALL_OBS)]),
     ):
         copy.wait()
-    out_ref[0 : FIELD + 4 * ROWS, :] = own_ref[...].astype(BF16)
-    out_ref[FIELD + 4 * ROWS : SENT_ROWS, :] = err_ref[...].astype(BF16)
+    both = own_ref[...].astype(BF16)
+    for out_ref, first in ((low_ref, 0), (high_ref, HALO)):
+        out_ref[0 : FIELD + 4 * ROWS, :] = both
+        for level in range(0, LEV, 4):
+            rows = [err_ref[(level + i) * ROWS + first : (level + i) * ROWS + first + HALO, :] for i in range(4)]
+            at = FIELD + 4 * ROWS + level * HALO
+            out_ref[at : at + 4 * HALO, :] = jnp.concatenate(rows, axis=0).astype(BF16)
 
 
 def widen(value):
@@ -153,8 +158,8 @@
     spread(low_tmp, south_ref[FIELD + 4 * ROWS :, :].astype(F32))
     spread(high_tmp, north_ref[FIELD + 4 * ROWS :, :].astype(F32))
     for row in range(HALO):
-        pack_ref[EXT + row] = spread_row(low_tmp, HALO + row)
-        pack_ref[EXT + HALO + row] = spread_row(high_tmp, row)
+        pack_ref[EXT + row] = spread_row(low_tmp, row, HALO)
+        pack_ref[EXT + HALO + row] = spread_row(high_tmp, row, HALO)
     spread(low_tmp, south_ref[0:FIELD, :].astype(F32))
     spread(high_tmp, north_ref[0:FIELD, :].astype(F32))
     for row in range(ROWS):
@@ -295,11 +300,11 @@
 
 
 def prepare_body(
-    next_ref, err_ref, dep_ref, pack_hbm, a_ref, b_ref, c_ref, d_ref, out_ref, *rest
+    next_ref, err_ref, pack_hbm, a_ref, b_ref, c_ref, d_ref, token_ref, *rest
 ):
     *coef_refs, own_tmp, pack_ref, sems = rest
     (wait,) = copies(sems, (pack_hbm, pack_ref))
-    out_ref[...] = dep_ref[...]
+    token_ref[...] = err_ref[:8, :BLK]
     spread(own_tmp, err_ref[...])
     wait.wait()
     final = lax.axis_index("tm") == lax.axis_size("tm") - 1
@@ -406,10 +411,11 @@
 
     err = error_weight.reshape(fields, LON)
     stencil = neighbor_weights.reshape(4 * ROWS, LON)
-    edge, own, aux = pl.pallas_call(
+    low, high, own, aux = pl.pallas_call(
         edges_body,
         in_specs=[home] * 5,
         out_shape=(
+            shape((SENT_ROWS, LON), BF16),
             shape((SENT_ROWS, LON), BF16),
             shape((FIELD + 4 * ROWS, LON), F32),
             shape((2 * ALL_OBS, BLK), F32),
@@ -418,8 +424,8 @@
         name="edges",
         compiler_params=params(60),
     )(start, stencil, err, values.reshape(ALL_OBS, BLK), obs_weight.reshape(ALL_OBS, BLK))
-    south = lax.ppermute(edge, "space", [(i, i + 1) for i in range(parts - 1)])
-    north = lax.ppermute(edge, "space", [(i + 1, i) for i in range(parts - 1)])
+    south = lax.ppermute(high, "space", [(i, i + 1) for i in range(parts - 1)])
+    north = lax.ppermute(low, "space", [(i + 1, i) for i in range(parts - 1)])
 
     request, choice = pl.pallas_call(
         request_body,
@@ -482,8 +488,18 @@
     previous = lax.ppermute(last, "tm", [(i, i + 1) for i in range(windows - 1)])
     following = lax.ppermute(following, "tm", [(i + 1, i) for i in range(windows - 1)])
 
+    quarter = shape((4, LEV, WIDE), F32)
+    *ahead, token, c, e, w, n, q = pl.pallas_call(
+        prepare_body,
+        in_specs=[vmem] * 2 + [home],
+        out_shape=(*[quarter] * 4, mark, *[shape((EXT, WIDE), F32)] * 5),
+        scratch_shapes=[runs, pltpu.VMEM((EXT + ROWS + 10, LEV, WIDE), F32), sems((1,))],
+        name="prepare",
+        compiler_params=params(51.5),
+    )(following, err, pack)
+
     per_obs = shape((ALL_OBS, BLK), F32)
-    found, slots = pl.pallas_call(
+    departures, slots = pl.pallas_call(
         observe_body,
         in_specs=[vmem] + [home] * 3 + [anywhere],
         out_shape=(per_obs, shape((PARTS * SENT, BLK), BF16)),
@@ -494,22 +510,12 @@
             sems((2 + ALL_OBS // GROUP,)),
         ],
         name="observe",
-        compiler_params=params(53.75),
-    )(got, choice, aux, operators.reshape(ALL_OBS * BLK, BLK), following)
+        compiler_params=params(53.78),
+    )(got, choice, aux, operators.reshape(ALL_OBS * BLK, BLK), token)
     arrived = exchange(slots)
 
     half = shape((2 * BLOCKS, BLK), BF16)
     put = pl.pallas_call(put_body, out_shape=(half, half), name="put", compiler_params=params(16))(asked)
-    quarter = shape((4, LEV, WIDE), F32)
-    *ahead, departures, c, e, w, n, q = pl.pallas_call(
-        prepare_body,
-        in_specs=[vmem] * 3 + [home],
-        out_shape=(*[quarter] * 4, per_obs, *[shape((EXT, WIDE), F32)] * 5),
-        scratch_shapes=[runs, pltpu.VMEM((EXT + ROWS + 10, LEV, WIDE), F32), sems((1,))],
-        name="prepare",
-        compiler_params=params(51.5),
-    )(following, err, found, pack)
-
     gradient = pl.pallas_call(
         adjoint_body,
         in_specs=[vmem] * 13 + [home] * 3,

time: 77.3 us -> 75.3 us (0.974)
  blocking collectives: 18.7 us -> 0 us
  waiting for transfers between devices: 9.23 us -> 20.6 us
  starting transfers between devices: 24.4 us -> 31 us
  local copies, waits for them, and re-layouts: 1.74 us -> 0.01 us
    all_to_all x1 -> x0, blocking collectives: 18.7 us -> none  [exchange(): lax.all_to_all(block, 'space', split_axis=0, concat_axis=0, tiled=True)]
    all_to_all x2 -> x3, waiting for transfers between devices: 7.58 us -> 15.8 us  [exchange(): lax.all_to_all(block, 'space', split_axis=0, concat_axis=0, tiled=True)]
    all_to_all x2 -> x3, starting transfers between devices: 15.8 us -> 22.5 us  [exchange(): lax.all_to_all(block, 'space', split_axis=0, concat_axis=0, tiled=True)]
    ppermute x1, waiting for transfers between devices: 1.65 us -> 4.75 us  [local(): lax.ppermute(last, 'tm', [(i, i + 1) for i in range(windows - 1)])]
    unnamed x6 -> x2, local copies, waits for them, and re-layouts: 1.74 us -> 0.01 us
  transfers between devices with their start and end apart: 6 -> 7, of which waited for: 3 -> 4; matrix products, arithmetic and copies ran while one was open for 0% -> 0% of each run, Pallas kernels for 14% -> 14%
where the time goes in v3:
time: 75.3 us; the launch traced here: 74.8 us
  starting transfers between devices  31 us (41%)
  Pallas kernels  22.4 us (30%)
  waiting for transfers between devices  20.6 us (27%)
  between operations  0.77 us (1%)
    all_to_all x3, starting transfers between devices, exchange(): lax.all_to_all(block, 'space', split_axis=0, concat_axis=0, tiled=True)  22.5 us
    all_to_all x3, waiting for transfers between devices, exchange(): lax.all_to_all(block, 'space', split_axis=0, concat_axis=0, tiled=True)  15.8 us
    pallas_call x1, Pallas kernels, local(): pl.pallas_call(forward_body, in_specs=[home, vmem, vmem], out_shape=(*[sh...  6.5 us
    ppermute x1, waiting for transfers between devices, local(): lax.ppermute(last, 'tm', [(i, i + 1) for i in range(windows - 1)])  4.75 us
    pallas_call x1, Pallas kernels, local(): pl.pallas_call(observe_body, in_specs=[vmem] + [home] * 3 + [anywhere], o...  4.09 us
    pallas_call x1, Pallas kernels, local(): pl.pallas_call(adjoint_body, in_specs=[vmem] * 13 + [home] * 3, out_shape...  4.06 us
    ppermute x1, starting transfers between devices, local(): south = lax.ppermute(high, 'space', [(i, i + 1) for i in range(parts - 1)])  3.42 us
    pallas_call x1, Pallas kernels, local(): pl.pallas_call(edges_body, in_specs=[home] * 5, out_shape=(shape((SENT_RO...  2.47 us
  transfers between devices with their start and end apart: 7, of which 4 were waited for; matrix products, arithmetic and copies ran while one was open for 0% of the time, Pallas kernels for 14%

profile of v3, /device:TPU:320, one launch (start us, length us, event | category | flops | bytes accessed | tf_op | source)
XLA Modules:
  0.0 74.8 jit_solution(15542681622737198362)
XLA Ops:
  0.6 0.0 copy-start
  0.6 2.5 %edges.1 = (bf16[128,1440]{1,0:T(8,128)(2,1)}, bf16[128,1440]{1,0:T(8,128)(2,1)}, f32[96,1440]{1,0:T(8,128)}, f32[192,128]{1,0:T(8,128)}) custom-call(f32[64,1440]{1,0:T(8,128)} %bitcast.29, f32[32,1440]{1,0:T(8,128)} %bitcast.34, f32[64,1440]{1,0:T(8,128)} %bitcast.21, f32[96,128]{1,0:T(8,128)} %bitcast.35, f32[96,128]{1,0:T(8,128)} %bitcast.36), custom_call_target="tpu_custom_call" | custom-call | tf_op jit(solution)/shard_map/edges/pallas_call | solution.py:414
  3.1 3.4 %collective-permute-start = (bf16[128,1440]{1,0:T(8,128)(2,1)}, bf16[128,1440]{1,0:T(8,128)(2,1)S(1)}, u32[]{:S(2)}, u32[]{:S(2)}) collective-permute-start(bf16[128,1440]{1,0:T(8,128)(2,1)} %get-tuple-element.36), channel_id=1, source_target_pairs={{0,1},{1,2},{2,3},{3,4},{4,5},{5,6},{6,7},{7,8},{8,9},{9,10},{10,1... | collective-permute-start | bytes 1105928 | tf_op jit(solution)/shard_map/ppermute | solution.py:427
  6.5 1.3 %collective-permute-start.1 = (bf16[128,1440]{1,0:T(8,128)(2,1)}, bf16[128,1440]{1,0:T(8,128)(2,1)S(1)}, u32[]{:S(2)}, u32[]{:S(2)}) collective-permute-start(bf16[128,1440]{1,0:T(8,128)(2,1)} %get-tuple-element.37), channel_id=1, source_target_pairs={{1,0},{2,1},{3,2},{4,3},{5,4},{6,5},{7,6},{8,7},{9,8},{10,9},{11,1... | collective-permute-start | bytes 1105928 | tf_op jit(solution)/shard_map/ppermute | solution.py:428
  7.8 1.7 %request.1 = (s32[32,128]{1,0:T(8,128)}, bf16[960,128]{1,0:T(8,128)(2,1)}) custom-call(s32[4,1,24]{2,1,0:T(1,128)} %bitcast.38, s32[4,24]{1,0:T(4,128)} %bitcast.39, f32[192,128]{1,0:T(8,128)} %get-tuple-element.33._.aux_hbm), custom_call_target="tpu_custom_call" | custom-call | tf_op jit(solution)/shard_map/request/pallas_call | solution.py:430
  9.6 12.0 %all-to-all-start = ((s32[32,1,128]{2,1,0:T(1,128)}), s32[32,1,128]{2,1,0:T(1,128)S(1)}, u32[]{:S(2)}, u32[]{:S(2)}) async-start(s32[32,1,128]{2,1,0:T(1,128)} %bitcast.37), calls=%async_computation | async-start | bytes 32768 | tf_op jit(solution)/shard_map/all_to_all | solution.py:386
  21.5 0.0 collective-permute-done.south_ref
  21.5 0.0 collective-permute-done.1.north_ref
  21.5 6.5 %forward.1 = (bf16[720,128]{1,0:T(8,128)(2,1)S(1)}, bf16[720,128]{1,0:T(8,128)(2,1)S(1)}, bf16[720,128]{1,0:T(8,128)(2,1)S(1)}, bf16[720,128]{1,0:T(8,128)(2,1)S...) custom-call(f32[96,1440]{1,0:T(8,128)} %get-tuple-element.35.own_hbm, ...), custom_call_target="tpu_custom_call" | custom-call | tf_op jit(solution)/shard_map/forward/pallas_call | solution.py:445
  28.1 3.1 %all-to-all-done = s32[32,1,128]{2,1,0:T(1,128)S(1)} async-done(((s32[32,1,128]{2,1,0:T(1,128)}), s32[32,1,128]{2,1,0:T(1,128)S(1)}, u32[]{:S(2)}, u32[]{:S(2)}) %all-to-all-start) | async-done | bytes 16416 | tf_op jit(solution)/shard_map/all_to_all | solution.py:386
  31.2 1.0 %gather.1 = (bf16[256,128]{1,0:T(8,128)(2,1)}, f32[8,128]{1,0:T(8,128)S(1)}) custom-call(s32[32,128]{1,0:T(8,128)S(1)} %bitcast.26, bf16[720,128]{1,0:T(8,128)(2,1)S(1)} %get-tuple-element.38.t1_ref, bf16[720,128]{1,0:T(8,128)(2,1)S(1)} %get-tuple-element.39.t2_ref, bf16[720,128]{1,0:T(8,128)(2,1)S(1)} %get-tuple-element.40.t3_ref, ...), custom_call_target="tpu_custom_call" | custom-call | tf_op jit(solution)/shard_map/gather/pallas_call | solution.py:469
  32.2 0.6 hold.1
  32.8 1.9 %collective-permute-start.2 = (bf16[128,1440]{1,0:T(8,128)(2,1)S(1)}, bf16[128,1440]{1,0:T(8,128)(2,1)S(1)}, u32[]{:S(2)}, u32[]{:S(2)}) collective-permute-start(bf16[128,1440]{1,0:T(8,128)(2,1)S(1)} %get-tuple-element.47), channel_id=1, source_target_pairs={{32,0},{64,32},{96,64},{128,96},{160,128},{192,160},{224,192},{256... | collective-permute-start | bytes 1105928 | tf_op jit(solution)/shard_map/ppermute | solution.py:489
  34.7 6.7 %all-to-all-start.1 = ((bf16[32,8,128]{2,1,0:T(8,128)(2,1)}), bf16[32,8,128]{2,1,0:T(8,128)(2,1)S(1)}, u32[]{:S(2)}, u32[]{:S(2)}) async-start(bf16[32,8,128]{2,1,0:T(8,128)(2,1)} %bitcast.11), calls=%async_computation.1 | async-start | bytes 131072 | tf_op jit(solution)/shard_map/all_to_all | solution.py:386
  41.3 0.0 collective-permute-done.2.next_ref
  41.4 0.0 copy-done
  41.4 1.7 %prepare.1 = (f32[4,8,1536]{2,1,0:T(8,128)S(1)}, f32[4,8,1536]{2,1,0:T(8,128)S(1)}, f32[4,8,1536]{2,1,0:T(8,128)S(1)}, f32[4,8,1536]{2,1,0:T(8,128)S(1)}, f32[8,...) custom-call(bf16[128,1440]{1,0:T(8,128)(2,1)S(1)} %collective-permut, ...), custom_call_target="tpu_custom_call" | custom-call | tf_op jit(solution)/shard_map/prepare/pallas_call | solution.py:492
  43.1 8.2 %all-to-all-done.1 = bf16[32,8,128]{2,1,0:T(8,128)(2,1)S(1)} async-done(((bf16[32,8,128]{2,1,0:T(8,128)(2,1)}), bf16[32,8,128]{2,1,0:T(8,128)(2,1)S(1)}, u32[]{:S(2)}, u32[]{:S(2)}) %all-to-all-start.1) | async-done | bytes 65568 | tf_op jit(solution)/shard_map/all_to_all | solution.py:386
  51.3 4.1 %observe.1 = (f32[96,128]{1,0:T(8,128)}, bf16[768,128]{1,0:T(8,128)(2,1)}) custom-call(bf16[256,128]{1,0:T(8,128)(2,1)S(1)} %bitcast.25, bf16[960,128]{1,0:T(8,128)(2,1)} %get-tuple-element.43.choice_hbm, f32[192,128]{1,0:T(8,128)} %get-tuple-element.33._.aux_hbm, bf16[12288,128]{1,0:T(8,128)(2,1)} %bitcast.28, f32[8,128]{1,0:T(8,128)S(1)} %get-tuple-element.49._), custom_call_target="tpu_custom_call" | custom-call | tf_op jit(solution)/shard_map/observe/pallas_call | solution.py:502
  55.4 3.9 %all-to-all-start.2 = ((bf16[32,24,128]{2,1,0:T(8,128)(2,1)}), bf16[32,24,128]{2,1,0:T(8,128)(2,1)S(1)}, u32[]{:S(2)}, u32[]{:S(2)}) async-start(bf16[32,24,128]{2,1,0:T(8,128)(2,1)} %bitcast.33), calls=%async_computation.2 | async-start | bytes 393216 | tf_op jit(solution)/shard_map/all_to_all | solution.py:386
  59.3 1.9 %collective-permute-start.3 = (bf16[64,1440]{1,0:T(8,128)(2,1)S(1)}, bf16[64,1440]{1,0:T(8,128)(2,1)S(1)}, u32[]{:S(2)}, u32[]{:S(2)}) collective-permute-start(bf16[64,1440]{1,0:T(8,128)(2,1)S(1)} %get-tuple-element.51), channel_id=1, source_target_pairs={{0,32},{32,64},{64,96},{96,128},{128,160},{160,192},{192,224},{224... | collective-permute-start | bytes 552968 | tf_op jit(solution)/shard_map/ppermute | solution.py:488
  61.2 0.3 put.1
  61.5 4.7 %collective-permute-done.3.prev_ref = bf16[64,1440]{1,0:T(8,128)(2,1)S(1)} collective-permute-done((bf16[64,1440]{1,0:T(8,128)(2,1)S(1)}, bf16[64,1440]{1,0:T(8,128)(2,1)S(1)}, u32[]{:S(2)}, u32[]{:S(2)}) %collective-permute-start.3) | collective-permute-done | bytes 184352 | tf_op jit(solution)/shard_map/ppermute | solution.py:488
  66.3 4.5 %all-to-all-done.2 = bf16[32,24,128]{2,1,0:T(8,128)(2,1)S(1)} async-done(((bf16[32,24,128]{2,1,0:T(8,128)(2,1)}), bf16[32,24,128]{2,1,0:T(8,128)(2,1)S(1)}, u32[]{:S(2)}, u32[]{:S(2)}) %all-to-all-start.2) | async-done | bytes 196640 | tf_op jit(solution)/shard_map/all_to_all | solution.py:386
  70.8 4.1 %adjoint.1 = f32[64,1440]{1,0:T(8,128)} custom-call(bf16[768,128]{1,0:T(8,128)(2,1)S(1)} %bitcast.24, bf16[64,1440]{1,0:T(8,128)(2,1)S(1)} %collective-permute-done.3.prev_ref, bf16[1440,128]{1,0:T(8,128)(2,1)S(1)} %get-tuple-element.52.late_ref, bf16[1440,128]{1,0:T(8,128)(2,1)S(1)} %get-tuple-element.53.early_ref, ...), custom_call_target="tpu_custom_call" | custom-call | tf_op jit(solution)/shard_map/adjoint/pallas_call | solution.py:519
Async XLA Ops:
  0.6 40.7 %copy-start = (f32[8,8,1440]{2,1,0:T(8,128)S(1)}, f32[8,8,1440]{2,1,0:T(8,128)}, u32[]{:S(2)}) copy-start(f32[8,8,1440]{2,1,0:T(8,128)} %param.11) | copy-start | bytes 1105924
  3.1 18.4 %collective-permute-start = (bf16[128,1440]{1,0:T(8,128)(2,1)}, bf16[128,1440]{1,0:T(8,128)(2,1)S(1)}, u32[]{:S(2)}, u32[]{:S(2)}) collective-permute-start(bf16[128,1440]{1,0:T(8,128)(2,1)} %get-tuple-element.36), channel_id=1, source_target_pairs={{0,1},{1,2},{2,3},{3,4},{4,5},{5,6},{6,7},{7,8},{8,9},{9,10},{10,1... | collective-permute-start | bytes 1105928 | tf_op jit(solution)/shard_map/ppermute | solution.py:427
  6.5 15.0 %collective-permute-start.1 = (bf16[128,1440]{1,0:T(8,128)(2,1)}, bf16[128,1440]{1,0:T(8,128)(2,1)S(1)}, u32[]{:S(2)}, u32[]{:S(2)}) collective-permute-start(bf16[128,1440]{1,0:T(8,128)(2,1)} %get-tuple-element.37), channel_id=1, source_target_pairs={{1,0},{2,1},{3,2},{4,3},{5,4},{6,5},{7,6},{8,7},{9,8},{10,9},{11,1... | collective-permute-start | bytes 1105928 | tf_op jit(solution)/shard_map/ppermute | solution.py:428
  9.6 21.6 %all-to-all-start = ((s32[32,1,128]{2,1,0:T(1,128)}), s32[32,1,128]{2,1,0:T(1,128)S(1)}, u32[]{:S(2)}, u32[]{:S(2)}) async-start(s32[32,1,128]{2,1,0:T(1,128)} %bitcast.37), calls=%async_computation | async-start | bytes 32768 | tf_op jit(solution)/shard_map/all_to_all | solution.py:386
  32.8 8.6 %collective-permute-start.2 = (bf16[128,1440]{1,0:T(8,128)(2,1)S(1)}, bf16[128,1440]{1,0:T(8,128)(2,1)S(1)}, u32[]{:S(2)}, u32[]{:S(2)}) collective-permute-start(bf16[128,1440]{1,0:T(8,128)(2,1)S(1)} %get-tuple-element.47), channel_id=1, source_target_pairs={{32,0},{64,32},{96,64},{128,96},{160,128},{192,160},{224,192},{256... | collective-permute-start | bytes 1105928 | tf_op jit(solution)/shard_map/ppermute | solution.py:489
  34.7 16.6 %all-to-all-start.1 = ((bf16[32,8,128]{2,1,0:T(8,128)(2,1)}), bf16[32,8,128]{2,1,0:T(8,128)(2,1)S(1)}, u32[]{:S(2)}, u32[]{:S(2)}) async-start(bf16[32,8,128]{2,1,0:T(8,128)(2,1)} %bitcast.11), calls=%async_computation.1 | async-start | bytes 131072 | tf_op jit(solution)/shard_map/all_to_all | solution.py:386
  55.4 15.4 %all-to-all-start.2 = ((bf16[32,24,128]{2,1,0:T(8,128)(2,1)}), bf16[32,24,128]{2,1,0:T(8,128)(2,1)S(1)}, u32[]{:S(2)}, u32[]{:S(2)}) async-start(bf16[32,24,128]{2,1,0:T(8,128)(2,1)} %bitcast.33), calls=%async_computation.2 | async-start | bytes 393216 | tf_op jit(solution)/shard_map/all_to_all | solution.py:386
  59.3 7.0 %collective-permute-start.3 = (bf16[64,1440]{1,0:T(8,128)(2,1)S(1)}, bf16[64,1440]{1,0:T(8,128)(2,1)S(1)}, u32[]{:S(2)}, u32[]{:S(2)}) collective-permute-start(bf16[64,1440]{1,0:T(8,128)(2,1)S(1)} %get-tuple-element.51), channel_id=1, source_target_pairs={{0,32},{32,64},{64,96},{96,128},{128,160},{160,192},{192,224},{224... | collective-permute-start | bytes 552968 | tf_op jit(solution)/shard_map/ppermute | solution.py:488

commit v4 on v3

--- a/solution.py
+++ b/solution.py
@@ -212,7 +212,7 @@
     last_ref[...] = gathered(own_tmp).astype(BF16)
 
 
-def gather_body(asked_ref, t1_ref, t2_ref, t3_ref, t4_ref, out_ref, token_ref, slots_ref):
+def gather_body(asked_ref, t1_ref, t2_ref, t3_ref, t4_ref, last_in, next_in, out_ref, last_out, next_out, slots_ref):
     lane = iota((PARTS, BLOCKS), 1)
     asked = asked_ref[...]
     for step in range(STEPS):
@@ -224,11 +224,6 @@
         for nth in range(2):
             slots_ref[pl.ds(2 * step + nth, PARTS, stride=SLOTS), :] = blocks[nth * PARTS : (nth + 1) * PARTS]
     out_ref[...] = slots_ref[...].astype(BF16)
-    token_ref[...] = slots_ref[0:8, :]
-
-
-def hold_body(token_ref, last_in, next_in, last_out, next_out, seen_ref):
-    seen_ref[...] = token_ref[...]
 
 
 def spread_out(block):
@@ -466,25 +461,18 @@
     )(own, south, north)
 
     mark = shape((8, BLK), F32)
-    blocks, token = pl.pallas_call(
+    blocks, last, following = pl.pallas_call(
         gather_body,
-        out_shape=(shape((PARTS * SLOTS, BLK), BF16), mark),
+        in_specs=[vmem] * 5 + [anywhere] * 2,
+        out_specs=(vmem, anywhere, anywhere),
+        out_shape=(shape((PARTS * SLOTS, BLK), BF16), here, around),
+        input_output_aliases={5: 1, 6: 2},
         scratch_shapes=[pltpu.VMEM((PARTS * SLOTS, BLK), F32)],
         name="gather",
         compiler_params=params(16),
-    )(asked, *tables)
+    )(asked, *tables, last, following)
     got = exchange(blocks)
 
-    last, following, token = pl.pallas_call(
-        hold_body,
-        in_specs=[vmem, anywhere, anywhere],
-        out_specs=(anywhere, anywhere, vmem),
-        out_shape=(here, around, mark),
-        input_output_aliases={1: 0, 2: 1},
-        name="hold",
-        cost_estimate=pl.CostEstimate(flops=0, transcendentals=0, bytes_accessed=30_000_000),
-        compiler_params=params(16),
-    )(token, last, following)
     previous = lax.ppermute(last, "tm", [(i, i + 1) for i in range(windows - 1)])
     following = lax.ppermute(following, "tm", [(i + 1, i) for i in range(windows - 1)])
 

time: 75.3 us -> 74.8 us (level)
    pallas_call x2 -> x1, Pallas kernels: 1.56 us -> 0.97 us  [local(): pl.pallas_call(gather_body, in_specs=[vmem] * 5 + [anywhere] * 2, out_spe...]
where the time goes in v4:
time: 74.8 us; the launch traced here: 74.2 us
  starting transfers between devices  31 us (41%)
  Pallas kernels  21.8 us (29%)
  waiting for transfers between devices  20.6 us (28%)
  between operations  0.77 us (1%)
    all_to_all x3, starting transfers between devices, exchange(): lax.all_to_all(block, 'space', split_axis=0, concat_axis=0, tiled=True)  22.5 us
    all_to_all x3, waiting for transfers between devices, exchange(): lax.all_to_all(block, 'space', split_axis=0, concat_axis=0, tiled=True)  15.8 us
    pallas_call x1, Pallas kernels, local(): pl.pallas_call(forward_body, in_specs=[home, vmem, vmem], out_shape=(*[sh...  6.5 us
    ppermute x1, waiting for transfers between devices, local(): lax.ppermute(last, 'tm', [(i, i + 1) for i in range(windows - 1)])  4.75 us
    pallas_call x1, Pallas kernels, local(): pl.pallas_call(observe_body, in_specs=[vmem] + [home] * 3 + [anywhere], o...  4.1 us
    pallas_call x1, Pallas kernels, local(): pl.pallas_call(adjoint_body, in_specs=[vmem] * 13 + [home] * 3, out_shape...  4.06 us
    ppermute x1, starting transfers between devices, local(): south = lax.ppermute(high, 'space', [(i, i + 1) for i in range(parts - 1)])  3.42 us
    pallas_call x1, Pallas kernels, local(): pl.pallas_call(edges_body, in_specs=[home] * 5, out_shape=(shape((SENT_RO...  2.47 us
  transfers between devices with their start and end apart: 7, of which 4 were waited for; matrix products, arithmetic and copies ran while one was open for 0% of the time, Pallas kernels for 14%

profile of v4, /device:TPU:320, one launch (start us, length us, event | category | flops | bytes accessed | tf_op | source)
XLA Modules:
  0.0 74.2 jit_solution(12761576216242131487)
XLA Ops:
  0.6 0.0 copy-start
  0.6 2.5 %edges.1 = (bf16[128,1440]{1,0:T(8,128)(2,1)}, bf16[128,1440]{1,0:T(8,128)(2,1)}, f32[96,1440]{1,0:T(8,128)}, f32[192,128]{1,0:T(8,128)}) custom-call(f32[64,1440]{1,0:T(8,128)} %bitcast.29, f32[32,1440]{1,0:T(8,128)} %bitcast.34, f32[64,1440]{1,0:T(8,128)} %bitcast.21, f32[96,128]{1,0:T(8,128)} %bitcast.35, f32[96,128]{1,0:T(8,128)} %bitcast.36), custom_call_target="tpu_custom_call" | custom-call | tf_op jit(solution)/shard_map/edges/pallas_call | solution.py:409
  3.1 3.4 %collective-permute-start = (bf16[128,1440]{1,0:T(8,128)(2,1)}, bf16[128,1440]{1,0:T(8,128)(2,1)S(1)}, u32[]{:S(2)}, u32[]{:S(2)}) collective-permute-start(bf16[128,1440]{1,0:T(8,128)(2,1)} %get-tuple-element.35), channel_id=1, source_target_pairs={{0,1},{1,2},{2,3},{3,4},{4,5},{5,6},{6,7},{7,8},{8,9},{9,10},{10,1... | collective-permute-start | bytes 1105928 | tf_op jit(solution)/shard_map/ppermute | solution.py:422
  6.5 1.3 %collective-permute-start.1 = (bf16[128,1440]{1,0:T(8,128)(2,1)}, bf16[128,1440]{1,0:T(8,128)(2,1)S(1)}, u32[]{:S(2)}, u32[]{:S(2)}) collective-permute-start(bf16[128,1440]{1,0:T(8,128)(2,1)} %get-tuple-element.36), channel_id=1, source_target_pairs={{1,0},{2,1},{3,2},{4,3},{5,4},{6,5},{7,6},{8,7},{9,8},{10,9},{11,1... | collective-permute-start | bytes 1105928 | tf_op jit(solution)/shard_map/ppermute | solution.py:423
  7.8 1.7 %request.1 = (s32[32,128]{1,0:T(8,128)}, bf16[960,128]{1,0:T(8,128)(2,1)}) custom-call(s32[4,1,24]{2,1,0:T(1,128)} %bitcast.38, s32[4,24]{1,0:T(4,128)} %bitcast.39, f32[192,128]{1,0:T(8,128)} %get-tuple-element.32._.aux_hbm), custom_call_target="tpu_custom_call" | custom-call | tf_op jit(solution)/shard_map/request/pallas_call | solution.py:425
  9.6 12.0 %all-to-all-start = ((s32[32,1,128]{2,1,0:T(1,128)}), s32[32,1,128]{2,1,0:T(1,128)S(1)}, u32[]{:S(2)}, u32[]{:S(2)}) async-start(s32[32,1,128]{2,1,0:T(1,128)} %bitcast.37), calls=%async_computation | async-start | bytes 32768 | tf_op jit(solution)/shard_map/all_to_all | solution.py:381
  21.5 0.0 collective-permute-done.south_ref
  21.5 0.0 collective-permute-done.1.north_ref
  21.6 6.5 %forward.1 = (bf16[720,128]{1,0:T(8,128)(2,1)S(1)}, bf16[720,128]{1,0:T(8,128)(2,1)S(1)}, bf16[720,128]{1,0:T(8,128)(2,1)S(1)}, bf16[720,128]{1,0:T(8,128)(2,1)S...) custom-call(f32[96,1440]{1,0:T(8,128)} %get-tuple-element.34.own_hbm, ...), custom_call_target="tpu_custom_call" | custom-call | tf_op jit(solution)/shard_map/forward/pallas_call | solution.py:440
  28.1 3.1 %all-to-all-done = s32[32,1,128]{2,1,0:T(1,128)S(1)} async-done(((s32[32,1,128]{2,1,0:T(1,128)}), s32[32,1,128]{2,1,0:T(1,128)S(1)}, u32[]{:S(2)}, u32[]{:S(2)}) %all-to-all-start) | async-done | bytes 16416 | tf_op jit(solution)/shard_map/all_to_all | solution.py:381
  31.2 1.0 %gather.1 = (bf16[256,128]{1,0:T(8,128)(2,1)}, bf16[64,1440]{1,0:T(8,128)(2,1)S(1)}, bf16[128,1440]{1,0:T(8,128)(2,1)S(1)}) custom-call(s32[32,128]{1,0:T(8,128)S(1)} %bitcast.26, bf16[720,128]{1,0:T(8,128)(2,1)S(1)} %get-tuple-element.37.t1_ref, bf16[720,128]{1,0:T(8,128)(2,1)S(1)} %get-tuple-element.38.t2_ref, ...), custom_call_target="tpu_custom_call", output_to_operand_aliasing={{1}: (5, {}), {2}: (6, {})} | custom-call | tf_op jit(solution)/shard_map/gather/pallas_call | solution.py:464
  32.2 1.9 %collective-permute-start.2 = (bf16[128,1440]{1,0:T(8,128)(2,1)S(1)}, bf16[128,1440]{1,0:T(8,128)(2,1)S(1)}, u32[]{:S(2)}, u32[]{:S(2)}) collective-permute-start(bf16[128,1440]{1,0:T(8,128)(2,1)S(1)} %get-tuple-element.45), channel_id=1, source_target_pairs={{32,0},{64,32},{96,64},{128,96},{160,128},{192,160},{224,192},{256... | collective-permute-start | bytes 1105928 | tf_op jit(solution)/shard_map/ppermute | solution.py:477
  34.1 6.7 %all-to-all-start.1 = ((bf16[32,8,128]{2,1,0:T(8,128)(2,1)}), bf16[32,8,128]{2,1,0:T(8,128)(2,1)S(1)}, u32[]{:S(2)}, u32[]{:S(2)}) async-start(bf16[32,8,128]{2,1,0:T(8,128)(2,1)} %bitcast.11), calls=%async_computation.1 | async-start | bytes 131072 | tf_op jit(solution)/shard_map/all_to_all | solution.py:381
  40.8 0.0 collective-permute-done.2.next_ref
  40.8 0.0 copy-done
  40.8 1.7 %prepare.1 = (f32[4,8,1536]{2,1,0:T(8,128)S(1)}, f32[4,8,1536]{2,1,0:T(8,128)S(1)}, f32[4,8,1536]{2,1,0:T(8,128)S(1)}, f32[4,8,1536]{2,1,0:T(8,128)S(1)}, f32[8,...) custom-call(bf16[128,1440]{1,0:T(8,128)(2,1)S(1)} %collective-permut, ...), custom_call_target="tpu_custom_call" | custom-call | tf_op jit(solution)/shard_map/prepare/pallas_call | solution.py:480
  42.5 8.2 %all-to-all-done.1 = bf16[32,8,128]{2,1,0:T(8,128)(2,1)S(1)} async-done(((bf16[32,8,128]{2,1,0:T(8,128)(2,1)}), bf16[32,8,128]{2,1,0:T(8,128)(2,1)S(1)}, u32[]{:S(2)}, u32[]{:S(2)}) %all-to-all-start.1) | async-done | bytes 65568 | tf_op jit(solution)/shard_map/all_to_all | solution.py:381
  50.7 4.1 %observe.1 = (f32[96,128]{1,0:T(8,128)}, bf16[768,128]{1,0:T(8,128)(2,1)}) custom-call(bf16[256,128]{1,0:T(8,128)(2,1)S(1)} %bitcast.25, bf16[960,128]{1,0:T(8,128)(2,1)} %get-tuple-element.44.choice_hbm, f32[192,128]{1,0:T(8,128)} %get-tuple-element.32._.aux_hbm, bf16[12288,128]{1,0:T(8,128)(2,1)} %bitcast.28, f32[8,128]{1,0:T(8,128)S(1)} %get-tuple-element.47._), custom_call_target="tpu_custom_call" | custom-call | tf_op jit(solution)/shard_map/observe/pallas_call | solution.py:490
  54.8 3.9 %all-to-all-start.2 = ((bf16[32,24,128]{2,1,0:T(8,128)(2,1)}), bf16[32,24,128]{2,1,0:T(8,128)(2,1)S(1)}, u32[]{:S(2)}, u32[]{:S(2)}) async-start(bf16[32,24,128]{2,1,0:T(8,128)(2,1)} %bitcast.33), calls=%async_computation.2 | async-start | bytes 393216 | tf_op jit(solution)/shard_map/all_to_all | solution.py:381
  58.7 1.9 %collective-permute-start.3 = (bf16[64,1440]{1,0:T(8,128)(2,1)S(1)}, bf16[64,1440]{1,0:T(8,128)(2,1)S(1)}, u32[]{:S(2)}, u32[]{:S(2)}) collective-permute-start(bf16[64,1440]{1,0:T(8,128)(2,1)S(1)} %get-tuple-element.49), channel_id=1, source_target_pairs={{0,32},{32,64},{64,96},{96,128},{128,160},{160,192},{192,224},{224... | collective-permute-start | bytes 552968 | tf_op jit(solution)/shard_map/ppermute | solution.py:476
  60.6 0.3 put.1
  61.0 4.7 %collective-permute-done.3.prev_ref = bf16[64,1440]{1,0:T(8,128)(2,1)S(1)} collective-permute-done((bf16[64,1440]{1,0:T(8,128)(2,1)S(1)}, bf16[64,1440]{1,0:T(8,128)(2,1)S(1)}, u32[]{:S(2)}, u32[]{:S(2)}) %collective-permute-start.3) | collective-permute-done | bytes 184352 | tf_op jit(solution)/shard_map/ppermute | solution.py:476
  65.7 4.5 %all-to-all-done.2 = bf16[32,24,128]{2,1,0:T(8,128)(2,1)S(1)} async-done(((bf16[32,24,128]{2,1,0:T(8,128)(2,1)}), bf16[32,24,128]{2,1,0:T(8,128)(2,1)S(1)}, u32[]{:S(2)}, u32[]{:S(2)}) %all-to-all-start.2) | async-done | bytes 196640 | tf_op jit(solution)/shard_map/all_to_all | solution.py:381
  70.2 4.1 %adjoint.1 = f32[64,1440]{1,0:T(8,128)} custom-call(bf16[768,128]{1,0:T(8,128)(2,1)S(1)} %bitcast.24, bf16[64,1440]{1,0:T(8,128)(2,1)S(1)} %collective-permute-done.3.prev_ref, bf16[1440,128]{1,0:T(8,128)(2,1)S(1)} %get-tuple-element.50.late_ref, bf16[1440,128]{1,0:T(8,128)(2,1)S(1)} %get-tuple-element.51.early_ref, ...), custom_call_target="tpu_custom_call" | custom-call | tf_op jit(solution)/shard_map/adjoint/pallas_call | solution.py:507
Async XLA Ops:
  0.6 40.1 %copy-start = (f32[8,8,1440]{2,1,0:T(8,128)S(1)}, f32[8,8,1440]{2,1,0:T(8,128)}, u32[]{:S(2)}) copy-start(f32[8,8,1440]{2,1,0:T(8,128)} %param.11) | copy-start | bytes 1105924
  3.1 18.4 %collective-permute-start = (bf16[128,1440]{1,0:T(8,128)(2,1)}, bf16[128,1440]{1,0:T(8,128)(2,1)S(1)}, u32[]{:S(2)}, u32[]{:S(2)}) collective-permute-start(bf16[128,1440]{1,0:T(8,128)(2,1)} %get-tuple-element.35), channel_id=1, source_target_pairs={{0,1},{1,2},{2,3},{3,4},{4,5},{5,6},{6,7},{7,8},{8,9},{9,10},{10,1... | collective-permute-start | bytes 1105928 | tf_op jit(solution)/shard_map/ppermute | solution.py:422
  6.5 15.0 %collective-permute-start.1 = (bf16[128,1440]{1,0:T(8,128)(2,1)}, bf16[128,1440]{1,0:T(8,128)(2,1)S(1)}, u32[]{:S(2)}, u32[]{:S(2)}) collective-permute-start(bf16[128,1440]{1,0:T(8,128)(2,1)} %get-tuple-element.36), channel_id=1, source_target_pairs={{1,0},{2,1},{3,2},{4,3},{5,4},{6,5},{7,6},{8,7},{9,8},{10,9},{11,1... | collective-permute-start | bytes 1105928 | tf_op jit(solution)/shard_map/ppermute | solution.py:423
  9.6 21.6 %all-to-all-start = ((s32[32,1,128]{2,1,0:T(1,128)}), s32[32,1,128]{2,1,0:T(1,128)S(1)}, u32[]{:S(2)}, u32[]{:S(2)}) async-start(s32[32,1,128]{2,1,0:T(1,128)} %bitcast.37), calls=%async_computation | async-start | bytes 32768 | tf_op jit(solution)/shard_map/all_to_all | solution.py:381
  32.2 8.6 %collective-permute-start.2 = (bf16[128,1440]{1,0:T(8,128)(2,1)S(1)}, bf16[128,1440]{1,0:T(8,128)(2,1)S(1)}, u32[]{:S(2)}, u32[]{:S(2)}) collective-permute-start(bf16[128,1440]{1,0:T(8,128)(2,1)S(1)} %get-tuple-element.45), channel_id=1, source_target_pairs={{32,0},{64,32},{96,64},{128,96},{160,128},{192,160},{224,192},{256... | collective-permute-start | bytes 1105928 | tf_op jit(solution)/shard_map/ppermute | solution.py:477
  34.1 16.6 %all-to-all-start.1 = ((bf16[32,8,128]{2,1,0:T(8,128)(2,1)}), bf16[32,8,128]{2,1,0:T(8,128)(2,1)S(1)}, u32[]{:S(2)}, u32[]{:S(2)}) async-start(bf16[32,8,128]{2,1,0:T(8,128)(2,1)} %bitcast.11), calls=%async_computation.1 | async-start | bytes 131072 | tf_op jit(solution)/shard_map/all_to_all | solution.py:381
  54.8 15.4 %all-to-all-start.2 = ((bf16[32,24,128]{2,1,0:T(8,128)(2,1)}), bf16[32,24,128]{2,1,0:T(8,128)(2,1)S(1)}, u32[]{:S(2)}, u32[]{:S(2)}) async-start(bf16[32,24,128]{2,1,0:T(8,128)(2,1)} %bitcast.33), calls=%async_computation.2 | async-start | bytes 393216 | tf_op jit(solution)/shard_map/all_to_all | solution.py:381
  58.7 7.0 %collective-permute-start.3 = (bf16[64,1440]{1,0:T(8,128)(2,1)S(1)}, bf16[64,1440]{1,0:T(8,128)(2,1)S(1)}, u32[]{:S(2)}, u32[]{:S(2)}) collective-permute-start(bf16[64,1440]{1,0:T(8,128)(2,1)S(1)} %get-tuple-element.49), channel_id=1, source_target_pairs={{0,32},{32,64},{64,96},{96,128},{128,160},{160,192},{192,224},{224... | collective-permute-start | bytes 552968 | tf_op jit(solution)/shard_map/ppermute | solution.py:476
